TPU v7x, 512 devices: a whole 4x4x16 slice. The times are simulated.
512 devices in a mesh: tm: 512 (over y, z, x, core).
Axes of the slice: x: 4, y: 4, z: 16, core: 2. Of those that a mesh axis runs over, the one named last changes fastest.
Arguments:
- trace: bfloat16 [262144, 512], P('tm'), may hold values from -6 to 6
- lengths: int32 [4], replicated, may hold values from 1 to 131072, as said below
- conv_weight: bfloat16 [2, 512, 1024], replicated, may hold values from -0.1875 to 0.1875
- res_weight: bfloat16 [512, 512], replicated, may hold values from -0.25 to 0.25
- cotangent: bfloat16 [262144, 512], P('tm'), may hold values from -6 to 6
Outputs:
- result: bfloat16 [262144, 512], P('tm')
- grad_input: bfloat16 [262144, 512], P('tm')
Inputs may be any that keep to these rules, and one draw needn't show every extreme that they name: The 4 traces lie end to end from time 0 in this order and their lengths sum to 262144.
All inputs are finite; a program needn't handle non-finite values.
Results may differ from a plain program's by a relative error of at most 0.003.
Values may be sent and summed in bfloat16 or wider, within the bound.
No kernel may reach another device: no remote copies, remote signals or barrier semaphores. Data moves between devices by JAX's collectives and lax.ppermute only.
A program may use at most 64 MiB of HBM per device.

v0:
```python
import jax
import jax.numpy as jnp
from jax import lax
from jax.sharding import PartitionSpec as P


def from_behind(value, axis, steps):
    count = lax.axis_size(axis)
    initial, last = (max(0, -steps), min(count, count - steps))
    return lax.ppermute(value, axis, [(source, source + steps) for source in range(initial, last)])


def per_device(trace, lengths, conv_weight, res_weight, cotangent):
    row_count = trace.shape[0]
    shard_gap = lax.axis_size("tm") // 8
    reach_rows = row_count * shard_gap
    sample_positions = lax.axis_index("tm") * row_count + lax.iota(jnp.int32, row_count)
    row_starts = jnp.cumsum(lengths) - lengths
    total_len = jnp.sum(lengths)
    half_width = conv_weight.shape[2] // 2
    trace_begin = jnp.max(
        jnp.where(row_starts[None, :] <= sample_positions[:, None], row_starts[None, :], 0), axis=1
    )
    inside = sample_positions < total_len
    delayed_mask = inside & (sample_positions - reach_rows >= trace_begin)
    delayed_rows = from_behind(trace, "tm", shard_gap)
    delayed_rows = jnp.where(delayed_mask[:, None], delayed_rows, jnp.zeros_like(delayed_rows))
    preact = jnp.dot(delayed_rows, conv_weight[0], preferred_element_type=jnp.float32)
    preact = preact + jnp.dot(trace, conv_weight[1], preferred_element_type=jnp.float32)
    filt_tanh = jnp.tanh(preact[:, :half_width])
    gate_sig = jax.nn.sigmoid(preact[:, half_width:])
    valid_f = inside.astype(jnp.float32)[:, None]
    mixed = (filt_tanh * gate_sig * valid_f).astype(jnp.bfloat16)
    output = (
        trace.astype(jnp.float32) + jnp.dot(mixed, res_weight, preferred_element_type=jnp.float32)
    ).astype(jnp.bfloat16)
    contract = (((1,), (1,)), ((), ()))
    grad_mix = (
        lax.dot_general(cotangent, res_weight, contract, preferred_element_type=jnp.float32)
        * valid_f
    )
    grad_filt = grad_mix * gate_sig * (1.0 - filt_tanh * filt_tanh)
    grad_gate = grad_mix * filt_tanh * gate_sig * (1.0 - gate_sig)
    grad_pre = jnp.concatenate([grad_filt, grad_gate], axis=1).astype(jnp.bfloat16)
    local_back = lax.dot_general(
        grad_pre, conv_weight[1], contract, preferred_element_type=jnp.float32
    )
    own_partial = lax.dot_general(
        grad_pre, conv_weight[0], contract, preferred_element_type=jnp.float32
    )
    own_partial = jnp.where(delayed_mask[:, None], own_partial, 0.0).astype(jnp.bfloat16)
    partial_output = from_behind(own_partial, "tm", -shard_gap)
    grad_input = (
        cotangent.astype(jnp.float32) + local_back + partial_output.astype(jnp.float32)
    ).astype(jnp.bfloat16)
    return (output, grad_input)


def solution(mesh):
    in_specs = (P("tm", None), P(), P(), P(), P("tm", None))
    out_specs = (P("tm", None), P("tm", None))
    return jax.shard_map(
        per_device, mesh=mesh, in_specs=in_specs, out_specs=out_specs, check_vma=False
    )
```

profile of v0, /device:TPU:46, one launch (start us, length us, event | category | flops | bytes accessed | tf_op | source)
XLA Modules:
  0.0 119.1 jit_solution(12784583365476426038)
XLA Ops:
  0.6 0.0 copy-start
  0.6 0.0 copy-start.1
  0.7 15.0 %collective-permute-start = (bf16[512,512]{1,0:T(8,128)(2,1)}, bf16[512,512]{1,0:T(8,128)(2,1)S(1)}, u32[]{:S(2)}, u32[]{:S(2)}) collective-permute-start(bf16[512,512]{1,0:T(8,128)(2,1)} %param.5), channel_id=1, source_target_pairs={{0,64},{1,65},{2,66},{3,67},{4,68},{5,69},{6,70},{7,71},{8,72},{9,... | collective-permute-start | bytes 1572872 | tf_op jit(solution)/shard_map/ppermute | solution.py:10
  15.6 0.8 reduce-window.9
  16.5 1.3 %fusion.27 = (s32[]{:T(128)}, s32[4]{0:T(128)S(1)}) fusion(s32[4]{0:T(128)} %param.6, s32[4,1]{0,1:T(1,128)S(1)} %reduce-window.9), kind=kLoop, calls=%fused_computation.40 | loop fusion | flops 7 | bytes 52 | tf_op jit(solution)/shard_map/reduce_sum | solution.py:19
  17.8 0.1 select_reduce_fusion
  17.8 0.7 fusion.20
  18.5 2.1 %fusion.6 = f32[512,1024]{1,0:T(8,128)S(1)} fusion(bf16[512,512]{1,0:T(8,128)(2,1)} %param.5, bf16[2,512,1024]{2,1,0:T(8,128)(2,1)} %param.7), kind=kOutput, calls=%fused_computation.14 | convolution fusion | flops 536870912 | bytes 3670016 | tf_op jit(solution)/shard_map/dot_general | solution.py:29
  20.6 38.7 %collective-permute-done = bf16[512,512]{1,0:T(8,128)(2,1)S(1)} collective-permute-done((bf16[512,512]{1,0:T(8,128)(2,1)}, bf16[512,512]{1,0:T(8,128)(2,1)S(1)}, u32[]{:S(2)}, u32[]{:S(2)}) %collective-permute-start) | collective-permute-done | bytes 524320 | tf_op jit(solution)/shard_map/ppermute | solution.py:10
  59.3 0.0 copy-done.1
  59.3 0.0 copy-start.3
  59.3 0.8 convolution_add_fusion
  60.1 0.0 copy-done
  60.1 0.2 copy-done.3
  60.4 0.8 multiply_convert_fusion.1
  61.2 0.0 copy-start.2
  61.2 0.8 fusion
  62.0 14.6 %collective-permute-start.1 = (bf16[512,512]{1,0:T(8,128)(2,1)S(1)}, bf16[512,512]{1,0:T(8,128)(2,1)S(1)}, u32[]{:S(2)}, u32[]{:S(2)}) collective-permute-start(bf16[512,512]{1,0:T(8,128)(2,1)S(1)} %fusion), channel_id=1, source_target_pairs={{64,0},{65,1},{66,2},{67,3},{68,4},{69,5},{70,6},{71,7},{72,8},{73... | collective-permute-start | bytes 1572872 | tf_op jit(solution)/shard_map/ppermute | solution.py:10
  76.6 0.0 copy-done.2
  76.6 1.5 %fusion.1 = bf16[512,512]{1,0:T(8,128)(2,1)} fusion(bf16[512,512]{1,0:T(8,128)(2,1)S(1)} %copy-done, bf16[512,512]{1,0:T(8,128)(2,1)S(1)} %copy-done.2, f32[512,1024]{1,0:T(8,128)S(1)} %convolution_add_fusion, f32[512]{0:T(512)S(1)} %get-tuple-element.7), kind=kOutput, calls=%fused_computation.6 | convolution fusion | flops 270794752 | bytes 3672064 | tf_op jit(solution)/shard_map/dot_general | solution.py:35
  78.1 39.4 %collective-permute-done.1 = bf16[512,512]{1,0:T(8,128)(2,1)S(1)} collective-permute-done((bf16[512,512]{1,0:T(8,128)(2,1)S(1)}, bf16[512,512]{1,0:T(8,128)(2,1)S(1)}, u32[]{:S(2)}, u32[]{:S(2)}) %collective-permute-start.1) | collective-permute-done | bytes 524320 | tf_op jit(solution)/shard_map/ppermute | solution.py:10
  117.5 1.6 %add_convert_fusion = bf16[512,512]{1,0:T(8,128)(2,1)} fusion(bf16[512,512]{1,0:T(8,128)(2,1)S(1)} %collective-permute-done.1, bf16[512,512]{1,0:T(8,128)(2,1)S(1)} %copy-done.3, bf16[2,512,1024]{2,1,0:T(8,128)(2,1)S(1)} %copy-done.1, bf16[512,512]{1,0:T(8,128)(2,1)S(1)} %get-tuple-element.3, bf16[512,512]{1,0:T(8,128)(2,1)S(1)} %get-tuple-element.2), kind=kOutput, calls=%fused_computation.18 | convolution fusion | flops 540278784 | bytes 3670016 | tf_op jit(solution)/shard_map/dot_general | solution.py:45
  (1 shorter events, 0.0 us)
Async XLA Ops:
  0.6 59.5 %copy-start = (bf16[512,512]{1,0:T(8,128)(2,1)S(1)}, bf16[512,512]{1,0:T(8,128)(2,1)}, u32[]{:S(2)}) copy-start(bf16[512,512]{1,0:T(8,128)(2,1)} %param.8) | copy-start | bytes 1572868
  0.6 58.7 %copy-start.1 = (bf16[2,512,1024]{2,1,0:T(8,128)(2,1)S(1)}, bf16[2,512,1024]{2,1,0:T(8,128)(2,1)}, u32[]{:S(2)}) copy-start(bf16[2,512,1024]{2,1,0:T(8,128)(2,1)} %param.7) | copy-start | bytes 6291460
  0.7 58.7 %collective-permute-start = (bf16[512,512]{1,0:T(8,128)(2,1)}, bf16[512,512]{1,0:T(8,128)(2,1)S(1)}, u32[]{:S(2)}, u32[]{:S(2)}) collective-permute-start(bf16[512,512]{1,0:T(8,128)(2,1)} %param.5), channel_id=1, source_target_pairs={{0,64},{1,65},{2,66},{3,67},{4,68},{5,69},{6,70},{7,71},{8,72},{9,... | collective-permute-start | bytes 1572872 | tf_op jit(solution)/shard_map/ppermute | solution.py:10
  59.3 1.0 copy-start.3
  61.2 15.4 %copy-start.2 = (bf16[512,512]{1,0:T(8,128)(2,1)S(1)}, bf16[512,512]{1,0:T(8,128)(2,1)}, u32[]{:S(2)}) copy-start(bf16[512,512]{1,0:T(8,128)(2,1)} %param.5) | copy-start | bytes 1572868
  62.0 55.5 %collective-permute-start.1 = (bf16[512,512]{1,0:T(8,128)(2,1)S(1)}, bf16[512,512]{1,0:T(8,128)(2,1)S(1)}, u32[]{:S(2)}, u32[]{:S(2)}) collective-permute-start(bf16[512,512]{1,0:T(8,128)(2,1)S(1)} %fusion), channel_id=1, source_target_pairs={{64,0},{65,1},{66,2},{67,3},{68,4},{69,5},{70,6},{71,7},{72,8},{73... | collective-permute-start | bytes 1572872 | tf_op jit(solution)/shard_map/ppermute | solution.py:10
where the time goes:
time: 119 us
  waiting for transfers between devices  78.1 us (66%)
  starting transfers between devices  29.5 us (25%)
  matrix products  7.59 us (6%)
  other arithmetic  2.86 us (2%)
    ppermute x2, waiting for transfers between devices, from_behind(): lax.ppermute(value, axis, [(source, source + steps) for source in range(i...  78.1 us
    ppermute x2, starting transfers between devices, from_behind(): lax.ppermute(value, axis, [(source, source + steps) for source in range(i...  29.5 us
  transfers between devices with their start and end apart: 2, of which 2 were waited for; matrix products, arithmetic and copies ran while one was open for 5% of the time, Pallas kernels for 0%

commit v1 on v0

v1 whole, which is shorter than its diff:
```python
import jax
import jax.numpy as jnp
from jax import lax
from jax.sharding import PartitionSpec as P

CHUNKS = 2
CONTRACT = (((1,), (1,)), ((), ()))


def shift(value, axis, steps):
    count = lax.axis_size(axis)
    initial, last = (max(0, -steps), min(count, count - steps))
    return lax.ppermute(value, axis, [(source, source + steps) for source in range(initial, last)])


def per_device(trace, lengths, conv_weight, res_weight, cotangent):
    row_count = trace.shape[0]
    shard_gap = lax.axis_size("tm") // 8
    reach_rows = row_count * shard_gap
    half_width = conv_weight.shape[2] // 2
    size = row_count // CHUNKS
    parts = [slice(k * size, (k + 1) * size) for k in range(CHUNKS)]

    past = [shift(trace[part], "tm", shard_gap) for part in parts]

    positions = lax.axis_index("tm") * row_count + lax.broadcasted_iota(jnp.int32, (row_count, 1), 0)
    ends = [lengths[0]]
    for k in range(1, lengths.shape[0]):
        ends.append(ends[-1] + lengths[k])
    begin = jnp.zeros_like(positions)
    for k in range(lengths.shape[0] - 1):
        begin = jnp.where(ends[k] <= positions, jnp.maximum(begin, ends[k]), begin)
    inside = positions < ends[-1]
    tap = inside & (positions - reach_rows >= begin)
    valid = inside.astype(jnp.float32)

    here = jnp.dot(trace, conv_weight[1], preferred_element_type=jnp.float32)
    mix = lax.dot_general(cotangent, res_weight, CONTRACT, preferred_element_type=jnp.float32)

    outputs, locals_, partials = [], [], []
    for k, part in enumerate(parts):
        arrived, here_part, mix_part = past[k], here[part], mix[part]
        if k:
            arrived, here_part, mix_part, _ = lax.optimization_barrier(
                (arrived, here_part, mix_part, own)
            )
        delayed = jnp.where(tap[part], arrived, jnp.zeros_like(arrived))
        preact = jnp.dot(delayed, conv_weight[0], preferred_element_type=jnp.float32) + here_part
        filt_tanh = jnp.tanh(preact[:, :half_width])
        gate_sig = jax.nn.sigmoid(preact[:, half_width:])
        valid_f = valid[part]
        mixed = (filt_tanh * gate_sig * valid_f).astype(jnp.bfloat16)
        grad_mix = mix_part * valid_f
        grad_filt = grad_mix * gate_sig * (1.0 - filt_tanh * filt_tanh)
        grad_gate = grad_mix * filt_tanh * gate_sig * (1.0 - gate_sig)
        grad_pre = jnp.concatenate([grad_filt, grad_gate], axis=1).astype(jnp.bfloat16)
        own = lax.dot_general(grad_pre, conv_weight[0], CONTRACT, preferred_element_type=jnp.float32)
        own = jnp.where(tap[part], own, 0.0).astype(jnp.bfloat16)
        partials.append(shift(own, "tm", -shard_gap))
        outputs.append(
            (
                trace[part].astype(jnp.float32)
                + jnp.dot(mixed, res_weight, preferred_element_type=jnp.float32)
            ).astype(jnp.bfloat16)
        )
        back = lax.dot_general(grad_pre, conv_weight[1], CONTRACT, preferred_element_type=jnp.float32)
        locals_.append(cotangent[part].astype(jnp.float32) + back)
    grads = [
        (local + partial.astype(jnp.float32)).astype(jnp.bfloat16)
        for local, partial in zip(locals_, partials)
    ]
    return (jnp.concatenate(outputs, axis=0), jnp.concatenate(grads, axis=0))


def solution(mesh):
    in_specs = (P("tm", None), P(), P(), P(), P("tm", None))
    out_specs = (P("tm", None), P("tm", None))
    return jax.shard_map(
        per_device, mesh=mesh, in_specs=in_specs, out_specs=out_specs, check_vma=False
    )
```

time: 119 us -> 117 us (0.983)
  the two profiles are of different devices: /device:TPU:46 before, /device:TPU:62 now
where the time goes in v1:
time: 117 us; the launch traced here: 116 us
  waiting for transfers between devices  79.7 us (68%)
  starting transfers between devices  20.7 us (18%)
  matrix products  6.5 us (6%)
  between operations  3.98 us (3%)
  other arithmetic  2.97 us (3%)
  local copies, waits for them, and re-layouts  2.6 us (2%)
    ppermute x4, waiting for transfers between devices, shift(): lax.ppermute(value, axis, [(source, source + steps) for source in range(i...  79.7 us
    ppermute x4, starting transfers between devices, shift(): lax.ppermute(value, axis, [(source, source + steps) for source in range(i...  20.7 us
  transfers between devices with their start and end apart: 4, of which 3 were waited for; matrix products, arithmetic and copies ran while one was open for 8% of the time, Pallas kernels for 0%

profile of v1, /device:TPU:62, one launch (start us, length us, event | category | flops | bytes accessed | tf_op | source)
XLA Modules:
  0.0 116.4 jit_solution(3212958471732344320)
XLA Ops:
  0.6 0.0 copy-start
  0.6 1.1 fusion.45
  1.8 14.8 %collective-permute-start = (bf16[256,512]{1,0:T(8,128)(2,1)S(1)}, bf16[256,512]{1,0:T(8,128)(2,1)S(1)}, u32[]{:S(2)}, u32[]{:S(2)}) collective-permute-start(bf16[256,512]{1,0:T(8,128)(2,1)S(1)} %get-tuple-element.15), channel_id=1, source_target_pairs={{0,64},{1,65},{2,66},{3,67},{4,68},{5,69},{6,70},{7,71},{8,72},{9,... | collective-permute-start | bytes 786440 | tf_op jit(solution)/shard_map/ppermute | solution.py:13
  16.6 1.9 %collective-permute-start.1 = (bf16[256,512]{1,0:T(8,128)(2,1)S(1)}, bf16[256,512]{1,0:T(8,128)(2,1)S(1)}, u32[]{:S(2)}, u32[]{:S(2)}) collective-permute-start(bf16[256,512]{1,0:T(8,128)(2,1)S(1)} %get-tuple-element.16), channel_id=1, source_target_pairs={{0,64},{1,65},{2,66},{3,67},{4,68},{5,69},{6,70},{7,71},{8,72},{9,... | collective-permute-start | bytes 786440 | tf_op jit(solution)/shard_map/ppermute | solution.py:13
  18.5 1.4 %fusion.47 = (s32[1]{0:T(128)}, s32[1]{0:T(128)}, s32[1]{0:T(128)}, s32[1]{0:T(128)}) fusion(s32[4]{0:T(128)} %param.6), kind=kLoop, calls=%fused_computation.74 | loop fusion | bytes 32 | tf_op jit(solution)/shard_map/slice | solution.py:29
  23.1 0.7 compare_and_fusion
  23.8 0.0 copy-start.4
  23.8 2.2 %fusion.6 = f32[512,1024]{1,0:T(8,128)S(1)} fusion(bf16[512,512]{1,0:T(8,128)(2,1)} %param.5, bf16[2,512,1024]{2,1,0:T(8,128)(2,1)} %param.7), kind=kOutput, calls=%fused_computation.14 | convolution fusion | flops 536870912 | bytes 3670016 | tf_op jit(solution)/shard_map/dot_general | solution.py:37
  25.9 0.0 copy-start.1
  26.0 0.0 copy-start.2
  26.0 0.0 copy-done
  26.0 0.0 copy-done.4
  26.0 0.5 fusion.48
  26.5 62.0 %collective-permute-done = bf16[256,512]{1,0:T(8,128)(2,1)S(1)} collective-permute-done((bf16[256,512]{1,0:T(8,128)(2,1)S(1)}, bf16[256,512]{1,0:T(8,128)(2,1)S(1)}, u32[]{:S(2)}, u32[]{:S(2)}) %collective-permute-start) | collective-permute-done | bytes 262176 | tf_op jit(solution)/shard_map/ppermute | solution.py:13
  88.5 0.0 copy-done.1
  88.5 0.0 copy-done.2
  88.5 0.5 convolution_add_fusion.1
  89.0 0.3 multiply_convert_fusion.4
  89.3 0.0 copy-start.3
  89.4 0.5 fusion.2
  89.9 0.0 slice-start
  89.9 2.1 %collective-permute-start.2 = (bf16[256,512]{1,0:T(8,128)(2,1)S(1)}, bf16[256,512]{1,0:T(8,128)(2,1)S(1)}, u32[]{:S(2)}, u32[]{:S(2)}) collective-permute-start(bf16[256,512]{1,0:T(8,128)(2,1)S(1)} %fusion.2), channel_id=1, source_target_pairs={{64,0},{65,1},{66,2},{67,3},{68,4},{69,5},{70,6},{71,7},{72,8},{73... | collective-permute-start | bytes 786440 | tf_op jit(solution)/shard_map/ppermute | solution.py:13
  91.9 0.0 copy-done.3
  91.9 0.4 fusion
  92.4 3.7 %collective-permute-done.1 = bf16[256,512]{1,0:T(8,128)(2,1)S(1)} collective-permute-done((bf16[256,512]{1,0:T(8,128)(2,1)S(1)}, bf16[256,512]{1,0:T(8,128)(2,1)S(1)}, u32[]{:S(2)}, u32[]{:S(2)}) %collective-permute-start.1) | collective-permute-done | bytes 262176 | tf_op jit(solution)/shard_map/ppermute | solution.py:13
  96.1 0.0 slice-done
  96.1 0.5 convolution_add_fusion
  96.6 0.3 multiply_convert_fusion.1
  96.9 0.5 fusion.3
  97.4 1.9 %collective-permute-start.3 = (bf16[256,512]{1,0:T(8,128)(2,1)S(1)}, bf16[256,512]{1,0:T(8,128)(2,1)S(1)}, u32[]{:S(2)}, u32[]{:S(2)}) collective-permute-start(bf16[256,512]{1,0:T(8,128)(2,1)S(1)} %fusion.3), channel_id=1, source_target_pairs={{64,0},{65,1},{66,2},{67,3},{68,4},{69,5},{70,6},{71,7},{72,8},{73... | collective-permute-start | bytes 786440 | tf_op jit(solution)/shard_map/ppermute | solution.py:13
  99.4 0.4 fusion.1
  99.8 0.8 pad_maximum_fusion.1
  100.6 13.9 %collective-permute-done.3 = bf16[256,512]{1,0:T(8,128)(2,1)S(1)} collective-permute-done((bf16[256,512]{1,0:T(8,128)(2,1)S(1)}, bf16[256,512]{1,0:T(8,128)(2,1)S(1)}, u32[]{:S(2)}, u32[]{:S(2)}) %collective-permute-start.3) | collective-permute-done | bytes 262176 | tf_op jit(solution)/shard_map/ppermute | solution.py:13
  114.6 0.5 add_convert_fusion
  115.1 0.0 collective-permute-done.2
  115.1 0.5 add_convert_fusion.1
  115.6 0.8 pad_maximum_fusion.3
  (2 shorter events, 0.0 us)
Async XLA Ops:
  0.6 25.3 %copy-start = (bf16[512,512]{1,0:T(8,128)(2,1)S(1)}, bf16[512,512]{1,0:T(8,128)(2,1)}, u32[]{:S(2)}) copy-start(bf16[512,512]{1,0:T(8,128)(2,1)} %param.8) | copy-start | bytes 1572868
  1.8 86.7 %collective-permute-start = (bf16[256,512]{1,0:T(8,128)(2,1)S(1)}, bf16[256,512]{1,0:T(8,128)(2,1)S(1)}, u32[]{:S(2)}, u32[]{:S(2)}) collective-permute-start(bf16[256,512]{1,0:T(8,128)(2,1)S(1)} %get-tuple-element.15), channel_id=1, source_target_pairs={{0,64},{1,65},{2,66},{3,67},{4,68},{5,69},{6,70},{7,71},{8,72},{9,... | collective-permute-start | bytes 786440 | tf_op jit(solution)/shard_map/ppermute | solution.py:13
  16.6 79.5 %collective-permute-start.1 = (bf16[256,512]{1,0:T(8,128)(2,1)S(1)}, bf16[256,512]{1,0:T(8,128)(2,1)S(1)}, u32[]{:S(2)}, u32[]{:S(2)}) collective-permute-start(bf16[256,512]{1,0:T(8,128)(2,1)S(1)} %get-tuple-element.16), channel_id=1, source_target_pairs={{0,64},{1,65},{2,66},{3,67},{4,68},{5,69},{6,70},{7,71},{8,72},{9,... | collective-permute-start | bytes 786440 | tf_op jit(solution)/shard_map/ppermute | solution.py:13
  23.8 2.2 %copy-start.4 = (bf16[512,512]{1,0:T(8,128)(2,1)S(1)}, bf16[512,512]{1,0:T(8,128)(2,1)}, u32[]{:S(2)}) copy-start(bf16[512,512]{1,0:T(8,128)(2,1)} %param.9) | copy-start | bytes 1572868
  25.9 62.5 %copy-start.1 = (f32[512,1024]{1,0:T(8,128)}, f32[512,1024]{1,0:T(8,128)S(1)}, u32[]{:S(2)}) copy-start(f32[512,1024]{1,0:T(8,128)S(1)} %fusion.6) | copy-start | bytes 6291460
  26.0 62.5 %copy-start.2 = (bf16[2,512,1024]{2,1,0:T(8,128)(2,1)S(1)}, bf16[2,512,1024]{2,1,0:T(8,128)(2,1)}, u32[]{:S(2)}) copy-start(bf16[2,512,1024]{2,1,0:T(8,128)(2,1)} %param.7) | copy-start | bytes 6291460
  89.3 2.6 %copy-start.3 = (bf16[512,512]{1,0:T(8,128)(2,1)S(1)}, bf16[512,512]{1,0:T(8,128)(2,1)}, u32[]{:S(2)}) copy-start(bf16[512,512]{1,0:T(8,128)(2,1)} %param.5) | copy-start | bytes 1572868
  89.9 6.3 %slice-start = ((f32[512,1024]{1,0:T(8,128)}), f32[256,1024]{1,0:T(8,128)S(1)}, s32[]{:S(2)}) async-start(f32[512,1024]{1,0:T(8,128)} %copy-done.1), calls=%async_computation | async-start | bytes 2097152 | tf_op jit(solution)/shard_map/slice | solution.py:42
  89.9 25.2 %collective-permute-start.2 = (bf16[256,512]{1,0:T(8,128)(2,1)S(1)}, bf16[256,512]{1,0:T(8,128)(2,1)S(1)}, u32[]{:S(2)}, u32[]{:S(2)}) collective-permute-start(bf16[256,512]{1,0:T(8,128)(2,1)S(1)} %fusion.2), channel_id=1, source_target_pairs={{64,0},{65,1},{66,2},{67,3},{68,4},{69,5},{70,6},{71,7},{72,8},{73... | collective-permute-start | bytes 786440 | tf_op jit(solution)/shard_map/ppermute | solution.py:13
  97.4 17.1 %collective-permute-start.3 = (bf16[256,512]{1,0:T(8,128)(2,1)S(1)}, bf16[256,512]{1,0:T(8,128)(2,1)S(1)}, u32[]{:S(2)}, u32[]{:S(2)}) collective-permute-start(bf16[256,512]{1,0:T(8,128)(2,1)S(1)} %fusion.3), channel_id=1, source_target_pairs={{64,0},{65,1},{66,2},{67,3},{68,4},{69,5},{70,6},{71,7},{72,8},{73... | collective-permute-start | bytes 786440 | tf_op jit(solution)/shard_map/ppermute | solution.py:13

commit v2 on v1

--- a/solution.py
+++ b/solution.py
@@ -1,43 +1,94 @@
+import functools
+
 import jax
 import jax.numpy as jnp
 from jax import lax
+from jax.experimental import pallas as pl
+from jax.experimental.pallas import tpu as pltpu
 from jax.sharding import PartitionSpec as P
 
+BLOCKS = 8
 CHUNKS = 2
 CONTRACT = (((1,), (1,)), ((), ()))
 
-
-def shift(value, axis, steps):
-    count = lax.axis_size(axis)
-    initial, last = (max(0, -steps), min(count, count - steps))
-    return lax.ppermute(value, axis, [(source, source + steps) for source in range(initial, last)])
+ROUTES = (
+    ((0, 2, 3, 4), ((4, 6), (3, 7)), ((0, 1), (2, 3)), ((6, 5), (7, 4))),
+    ((0, 2, 3, 4, 6), ((3, 7),), ((0, 1), (2, 3), (4, 5), (6, 7)), ((7, 4),)),
+    ((1, 2, 3, 5), ((2, 0), (3, 5), (5, 7)), ((1, 2),), ((0, 3), (5, 4), (7, 6))),
+    ((1, 2, 3, 6), ((2, 0), (3, 5)), ((1, 2), (6, 7)), ((0, 3), (5, 4))),
+    (tuple(range(BLOCKS - 1)), (), tuple((i, i + 1) for i in range(BLOCKS - 1)), ()),
+)
 
 
-def per_device(trace, lengths, conv_weight, res_weight, cotangent):
+def route_kernel(gap, rows, me_ref, lengths_ref, out_ref):
+    position = lax.rem(me_ref[0], gap)
+    reach = gap * rows
+    starts = [lengths_ref[0]]
+    for k in range(1, lengths_ref.shape[0] - 1):
+        starts.append(starts[-1] + lengths_ref[k])
+    total = starts[-1] + lengths_ref[lengths_ref.shape[0] - 1]
+    live = []
+    for edge in range(BLOCKS - 1):
+        first = ((edge + 1) * gap + position) * rows
+        dead = first >= total
+        for start in starts:
+            dead = dead | ((start <= first) & (first + rows <= start + reach))
+        live.append(jnp.logical_not(dead))
+    choice = jnp.int32(len(ROUTES) - 1)
+    for k in reversed(range(len(ROUTES) - 1)):
+        missed = jnp.bool_(False)
+        for edge in range(BLOCKS - 1):
+            if edge not in ROUTES[k][0]:
+                missed = missed | live[edge]
+        choice = jnp.where(missed, choice, jnp.int32(k))
+    out_ref[0] = choice
+
+
+def choose_route(me, lengths, gap, rows):
+    smem = pl.BlockSpec(memory_space=pltpu.SMEM)
+    return pl.pallas_call(
+        functools.partial(route_kernel, gap, rows),
+        out_shape=jax.ShapeDtypeStruct((1,), jnp.int32),
+        in_specs=[smem, smem],
+        out_specs=smem,
+        name="route",
+    )(me.reshape(1), lengths)[0]
+
+
+def move(value, gap, hops):
+    return lax.ppermute(
+        value, "tm", [(a * gap + r, b * gap + r) for a, b in hops for r in range(gap)]
+    )
+
+
+def is_in(block, blocks):
+    found = jnp.bool_(False)
+    for b in blocks:
+        found = found | (block == b)
+    return found
+
+
+def layer(route, gap, block, trace, conv_weight, res_weight, cotangent, tap, valid):
+    edges, hops, own_sends, relay_sends = route
+    returns = tuple((i + 1, i) for i in edges)
     row_count = trace.shape[0]
-    shard_gap = lax.axis_size("tm") // 8
-    reach_rows = row_count * shard_gap
     half_width = conv_weight.shape[2] // 2
     size = row_count // CHUNKS
     parts = [slice(k * size, (k + 1) * size) for k in range(CHUNKS)]
 
-    past = [shift(trace[part], "tm", shard_gap) for part in parts]
-
-    positions = lax.axis_index("tm") * row_count + lax.broadcasted_iota(jnp.int32, (row_count, 1), 0)
-    ends = [lengths[0]]
-    for k in range(1, lengths.shape[0]):
-        ends.append(ends[-1] + lengths[k])
-    begin = jnp.zeros_like(positions)
-    for k in range(lengths.shape[0] - 1):
-        begin = jnp.where(ends[k] <= positions, jnp.maximum(begin, ends[k]), begin)
-    inside = positions < ends[-1]
-    tap = inside & (positions - reach_rows >= begin)
-    valid = inside.astype(jnp.float32)
+    if hops:
+        hopped = [move(trace[part], gap, hops) for part in parts]
+    past = [move(trace[part], gap, own_sends) for part in parts]
+    if hops:
+        relayed = [move(value, gap, relay_sends) for value in hopped]
+        by_relay = is_in(block, [b for _, b in relay_sends])
+        past = [jnp.where(by_relay, b, a) for a, b in zip(past, relayed)]
 
     here = jnp.dot(trace, conv_weight[1], preferred_element_type=jnp.float32)
     mix = lax.dot_general(cotangent, res_weight, CONTRACT, preferred_element_type=jnp.float32)
 
     outputs, locals_, partials = [], [], []
+    own = None
     for k, part in enumerate(parts):
         arrived, here_part, mix_part = past[k], here[part], mix[part]
         if k:
@@ -56,7 +107,7 @@
         grad_pre = jnp.concatenate([grad_filt, grad_gate], axis=1).astype(jnp.bfloat16)
         own = lax.dot_general(grad_pre, conv_weight[0], CONTRACT, preferred_element_type=jnp.float32)
         own = jnp.where(tap[part], own, 0.0).astype(jnp.bfloat16)
-        partials.append(shift(own, "tm", -shard_gap))
+        partials.append(move(own, gap, returns))
         outputs.append(
             (
                 trace[part].astype(jnp.float32)
@@ -72,6 +123,26 @@
     return (jnp.concatenate(outputs, axis=0), jnp.concatenate(grads, axis=0))
 
 
+def per_device(trace, lengths, conv_weight, res_weight, cotangent):
+    row_count = trace.shape[0]
+    gap = lax.axis_size("tm") // BLOCKS
+    me = lax.axis_index("tm")
+    choice = choose_route(me, lengths, gap, row_count)
+
+    positions = me * row_count + lax.broadcasted_iota(jnp.int32, (row_count, 1), 0)
+    ends = jnp.cumsum(lengths)
+    starts = ends - lengths
+    begin = jnp.max(jnp.where(starts[None, :] <= positions, starts[None, :], 0), axis=1, keepdims=True)
+    inside = positions < jnp.sum(lengths)
+    tap = inside & (positions - row_count * gap >= begin)
+    valid = inside.astype(jnp.float32)
+
+    branches = [functools.partial(layer, route, gap, me // gap) for route in ROUTES]
+    return lax.switch(
+        choice, branches, trace, conv_weight, res_weight, cotangent, tap, valid
+    )
+
+
 def solution(mesh):
     in_specs = (P("tm", None), P(), P(), P(), P("tm", None))
     out_specs = (P("tm", None), P("tm", None))

time: 117 us -> 126 us (1.077)
  the two profiles are of different devices: /device:TPU:62 before, /device:TPU:53 now
where the time goes in v2:
time: 126 us; the launch traced here: 125 us
  starting transfers between devices  60.8 us (48%)
  waiting for transfers between devices  46.2 us (37%)
  matrix products  7.76 us (6%)
  other arithmetic  5.23 us (4%)
  local copies, waits for them, and re-layouts  1.83 us (1%)
  between operations  1.48 us (1%)
    ppermute x8, starting transfers between devices, move(): lax.ppermute(value, 'tm', [(a * gap + r, b * gap + r) for a, b in hops fo...  60.8 us
    ppermute x8, waiting for transfers between devices, move(): lax.ppermute(value, 'tm', [(a * gap + r, b * gap + r) for a, b in hops fo...  46.2 us
    dot_general x1, matrix products, layer(): here = jnp.dot(trace, conv_weight[1], preferred_element_type=jnp.float32)  3.53 us
  transfers between devices with their start and end apart: 8, of which 2 were waited for; matrix products, arithmetic and copies ran while one was open for 7% of the time, Pallas kernels for 0%

profile of v2, /device:TPU:53, one launch (start us, length us, event | category | flops | bytes accessed | tf_op | source)
XLA Modules:
  0.0 125.2 jit_solution(1359406272455549676)
XLA Ops:
  0.6 1.2 route.1
  2.5 0.8 reduce-window.9
  3.3 1.3 %fusion.267 = (s32[]{:T(128)}, s32[4]{0:T(128)S(1)}) fusion(s32[4]{0:T(128)} %lengths_ref.1, s32[4,1]{0,1:T(1,128)S(1)} %reduce-window.9), kind=kLoop, calls=%fused_computation.362 | loop fusion | flops 7 | bytes 52 | tf_op jit(solution)/shard_map/reduce_sum | solution.py:136
  4.6 0.1 select_reduce_fusion
  4.7 0.7 compare_and_fusion
  5.4 119.7 %conditional.1 = (bf16[512,512]{1,0:T(8,128)(2,1)}, bf16[512,512]{1,0:T(8,128)(2,1)}) conditional(s32[]{:T(128)} %bitcast.21, (bf16[512,512]{1,0:T(8,128)(2,1)}, pred[512,1]{0,1:T(4,128)(4,1)S(1)}, s32[]{:T(128)}, bf16[2,512,1024]{2,1,0:T(8,128)(2,1)}, f32[512,1]{0,1:T(1,128)S(1)}, ...), branch_computations={%region_3.4_spmd, %region_4.5_spmd, %region_5.6_spmd, %region_6.7_... | conditional | flops 2699558912 | bytes 71315064 | solution.py:141
  5.4 1.8 %fusion.261 = (bf16[256,512]{1,0:T(8,128)(2,1)}, bf16[256,512]{1,0:T(8,128)(2,1)S(1)}) fusion(bf16[512,512]{1,0:T(8,128)(2,1)} %get-tuple-element.88), kind=kLoop, calls=%fused_computation.356 | loop fusion | bytes 1048576 | tf_op jit(solution)/shard_map/cond/branch_2_fun/slice | solution.py:113
  7.2 1.3 %collective-permute-start.16 = (bf16[256,512]{1,0:T(8,128)(2,1)}, bf16[256,512]{1,0:T(8,128)(2,1)}, u32[]{:S(2)}, u32[]{:S(2)}) collective-permute-start(bf16[256,512]{1,0:T(8,128)(2,1)} %get-tuple-element.218), channel_id=1, source_target_pairs={{128,0},{129,1},{130,2},{131,3},{132,4},{133,5},{134,6},{135,7},{1... | collective-permute-start | bytes 786440 | tf_op jit(solution)/shard_map/cond/branch_2_fun/ppermute | solution.py:59
  8.5 1.4 %collective-permute-start.18 = (bf16[256,512]{1,0:T(8,128)(2,1)}, bf16[256,512]{1,0:T(8,128)(2,1)}, u32[]{:S(2)}, u32[]{:S(2)}) collective-permute-start(bf16[256,512]{1,0:T(8,128)(2,1)} %get-tuple-element.218), channel_id=1, source_target_pairs={{64,128},{65,129},{66,130},{67,131},{68,132},{69,133},{70,134},{71... | collective-permute-start | bytes 786440 | tf_op jit(solution)/shard_map/cond/branch_2_fun/ppermute | solution.py:59
  9.9 1.4 %collective-permute-start.19 = (bf16[256,512]{1,0:T(8,128)(2,1)S(1)}, bf16[256,512]{1,0:T(8,128)(2,1)}, u32[]{:S(2)}, u32[]{:S(2)}) collective-permute-start(bf16[256,512]{1,0:T(8,128)(2,1)S(1)} %get-tuple-element.219), channel_id=1, source_target_pairs={{128,0},{129,1},{130,2},{131,3},{132,4},{133,5},{134,6},{135,7},{1... | collective-permute-start | bytes 786440 | tf_op jit(solution)/shard_map/cond/branch_2_fun/ppermute | solution.py:59
  11.2 1.4 %collective-permute-start.21 = (bf16[256,512]{1,0:T(8,128)(2,1)S(1)}, bf16[256,512]{1,0:T(8,128)(2,1)}, u32[]{:S(2)}, u32[]{:S(2)}) collective-permute-start(bf16[256,512]{1,0:T(8,128)(2,1)S(1)} %get-tuple-element.219), channel_id=1, source_target_pairs={{64,128},{65,129},{66,130},{67,131},{68,132},{69,133},{70,134},{71... | collective-permute-start | bytes 786440 | tf_op jit(solution)/shard_map/cond/branch_2_fun/ppermute | solution.py:59
  12.6 3.5 %fusion.112 = f32[512,1024]{1,0:T(8,128)} fusion(bf16[512,512]{1,0:T(8,128)(2,1)} %get-tuple-element.88, bf16[2,512,1024]{2,1,0:T(8,128)(2,1)} %get-tuple-element.91), kind=kOutput, calls=%fused_computation.153 | convolution fusion | flops 536870912 | bytes 3670016 | tf_op jit(solution)/shard_map/cond/branch_2_fun/dot_general | solution.py:87
  16.2 0.0 copy-start.2
  16.2 0.0 copy-start.25
  16.2 0.0 collective-permute-done.16
  16.2 1.6 %collective-permute-start.17 = (bf16[256,512]{1,0:T(8,128)(2,1)}, bf16[256,512]{1,0:T(8,128)(2,1)S(1)}, u32[]{:S(2)}, u32[]{:S(2)}) collective-permute-start(bf16[256,512]{1,0:T(8,128)(2,1)} %collective-permute-done.16), channel_id=1, source_target_pairs={{0,192},{1,193},{2,194},{3,195},{4,196},{5,197},{6,198},{7,199},{8... | collective-permute-start | bytes 786440 | tf_op jit(solution)/shard_map/cond/branch_2_fun/ppermute | solution.py:59
  17.8 0.0 copy-done.12
  17.8 0.0 copy-done.19
  17.8 0.5 fusion.270
  18.3 0.0 collective-permute-done.19
  18.3 1.3 %collective-permute-start.20 = (bf16[256,512]{1,0:T(8,128)(2,1)}, bf16[256,512]{1,0:T(8,128)(2,1)S(1)}, u32[]{:S(2)}, u32[]{:S(2)}) collective-permute-start(bf16[256,512]{1,0:T(8,128)(2,1)} %collective-permute-done.19), channel_id=1, source_target_pairs={{0,192},{1,193},{2,194},{3,195},{4,196},{5,197},{6,198},{7,199},{8... | collective-permute-start | bytes 786440 | tf_op jit(solution)/shard_map/cond/branch_2_fun/ppermute | solution.py:59
  19.6 0.0 collective-permute-done.18
  19.6 18.9 %collective-permute-done.17 = bf16[256,512]{1,0:T(8,128)(2,1)S(1)} collective-permute-done((bf16[256,512]{1,0:T(8,128)(2,1)}, bf16[256,512]{1,0:T(8,128)(2,1)S(1)}, u32[]{:S(2)}, u32[]{:S(2)}) %collective-permute-start.17) | collective-permute-done | bytes 262176 | tf_op jit(solution)/shard_map/cond/branch_2_fun/ppermute | solution.py:59
  38.5 0.0 copy-done.2
  38.5 0.0 copy-done.25
  38.5 0.5 convolution_add_fusion.10
  39.0 0.3 multiply_convert_fusion.20
  39.3 0.0 copy-start.7
  39.3 0.5 fusion.108
  39.8 0.0 slice-start.1
  39.8 45.0 %collective-permute-start.22 = (bf16[256,512]{1,0:T(8,128)(2,1)S(1)}, bf16[256,512]{1,0:T(8,128)(2,1)S(1)}, u32[]{:S(2)}, u32[]{:S(2)}) collective-permute-start(bf16[256,512]{1,0:T(8,128)(2,1)S(1)} %fusion.108), channel_id=1, source_target_pairs={{128,64},{129,65},{130,66},{131,67},{132,68},{133,69},{134,70},{13... | collective-permute-start | bytes 786440 | tf_op jit(solution)/shard_map/cond/branch_2_fun/ppermute | solution.py:59
  84.8 0.0 copy-done.7
  84.9 0.4 fusion.106
  85.3 0.0 collective-permute-done.21
  85.3 0.0 collective-permute-done.20
  85.3 0.1 broadcast_select_fusion.2
  85.4 0.5 fusion.138
  85.9 0.3 multiply_convert_fusion.17
  86.2 0.5 fusion.109
  86.7 0.0 copy-start.20
  86.7 7.5 %collective-permute-start.23 = (bf16[256,512]{1,0:T(8,128)(2,1)S(1)}, bf16[256,512]{1,0:T(8,128)(2,1)S(1)}, u32[]{:S(2)}, u32[]{:S(2)}) collective-permute-start(bf16[256,512]{1,0:T(8,128)(2,1)S(1)} %fusion.109), channel_id=1, source_target_pairs={{128,64},{129,65},{130,66},{131,67},{132,68},{133,69},{134,70},{13... | collective-permute-start | bytes 786440 | tf_op jit(solution)/shard_map/cond/branch_2_fun/ppermute | solution.py:59
  94.2 0.4 fusion.107
  94.7 0.8 pad_maximum_fusion.17
  95.5 27.3 %collective-permute-done.23 = bf16[256,512]{1,0:T(8,128)(2,1)S(1)} collective-permute-done((bf16[256,512]{1,0:T(8,128)(2,1)S(1)}, bf16[256,512]{1,0:T(8,128)(2,1)S(1)}, u32[]{:S(2)}, u32[]{:S(2)}) %collective-permute-start.23) | collective-permute-done | bytes 262176 | tf_op jit(solution)/shard_map/cond/branch_2_fun/ppermute | solution.py:59
  122.8 0.5 add_convert_fusion.4
  123.3 0.0 collective-permute-done.22
  123.3 0.5 add_convert_fusion.5
  123.8 0.8 pad_maximum_fusion.19
  (7 shorter events, 0.0 us)
Async XLA Ops:
  7.2 9.0 %collective-permute-start.16 = (bf16[256,512]{1,0:T(8,128)(2,1)}, bf16[256,512]{1,0:T(8,128)(2,1)}, u32[]{:S(2)}, u32[]{:S(2)}) collective-permute-start(bf16[256,512]{1,0:T(8,128)(2,1)} %get-tuple-element.218), channel_id=1, source_target_pairs={{128,0},{129,1},{130,2},{131,3},{132,4},{133,5},{134,6},{135,7},{1... | collective-permute-start | bytes 786440 | tf_op jit(solution)/shard_map/cond/branch_2_fun/ppermute | solution.py:59
  8.5 11.1 %collective-permute-start.18 = (bf16[256,512]{1,0:T(8,128)(2,1)}, bf16[256,512]{1,0:T(8,128)(2,1)}, u32[]{:S(2)}, u32[]{:S(2)}) collective-permute-start(bf16[256,512]{1,0:T(8,128)(2,1)} %get-tuple-element.218), channel_id=1, source_target_pairs={{64,128},{65,129},{66,130},{67,131},{68,132},{69,133},{70,134},{71... | collective-permute-start | bytes 786440 | tf_op jit(solution)/shard_map/cond/branch_2_fun/ppermute | solution.py:59
  9.9 8.4 %collective-permute-start.19 = (bf16[256,512]{1,0:T(8,128)(2,1)S(1)}, bf16[256,512]{1,0:T(8,128)(2,1)}, u32[]{:S(2)}, u32[]{:S(2)}) collective-permute-start(bf16[256,512]{1,0:T(8,128)(2,1)S(1)} %get-tuple-element.219), channel_id=1, source_target_pairs={{128,0},{129,1},{130,2},{131,3},{132,4},{133,5},{134,6},{135,7},{1... | collective-permute-start | bytes 786440 | tf_op jit(solution)/shard_map/cond/branch_2_fun/ppermute | solution.py:59
  11.2 74.1 %collective-permute-start.21 = (bf16[256,512]{1,0:T(8,128)(2,1)S(1)}, bf16[256,512]{1,0:T(8,128)(2,1)}, u32[]{:S(2)}, u32[]{:S(2)}) collective-permute-start(bf16[256,512]{1,0:T(8,128)(2,1)S(1)} %get-tuple-element.219), channel_id=1, source_target_pairs={{64,128},{65,129},{66,130},{67,131},{68,132},{69,133},{70,134},{71... | collective-permute-start | bytes 786440 | tf_op jit(solution)/shard_map/cond/branch_2_fun/ppermute | solution.py:59
  12.6 5.2 %copy-start.12 = (bf16[512,512]{1,0:T(8,128)(2,1)S(1)}, bf16[512,512]{1,0:T(8,128)(2,1)}, u32[]{:S(2)}) copy-start(bf16[512,512]{1,0:T(8,128)(2,1)} %get-tuple-element.93) | copy-start | bytes 1572868 | tf_op jit(solution)/shard_map/cond
  12.6 5.2 %copy-start.19 = (bf16[512,512]{1,0:T(8,128)(2,1)S(1)}, bf16[512,512]{1,0:T(8,128)(2,1)}, u32[]{:S(2)}) copy-start(bf16[512,512]{1,0:T(8,128)(2,1)} %get-tuple-element.94) | copy-start | bytes 1572868 | tf_op jit(solution)/shard_map/cond
  16.2 22.3 %copy-start.2 = (bf16[2,512,1024]{2,1,0:T(8,128)(2,1)S(1)}, bf16[2,512,1024]{2,1,0:T(8,128)(2,1)}, u32[]{:S(2)}) copy-start(bf16[2,512,1024]{2,1,0:T(8,128)(2,1)} %get-tuple-element.91) | copy-start | bytes 6291460 | tf_op jit(solution)/shard_map/cond
  16.2 22.3 %copy-start.25 = (f32[512,1024]{1,0:T(8,128)S(1)}, f32[512,1024]{1,0:T(8,128)}, u32[]{:S(2)}) copy-start(f32[512,1024]{1,0:T(8,128)} %fusion.112) | copy-start | bytes 6291460 | tf_op jit(solution)/shard_map/cond
  16.2 22.3 %collective-permute-start.17 = (bf16[256,512]{1,0:T(8,128)(2,1)}, bf16[256,512]{1,0:T(8,128)(2,1)S(1)}, u32[]{:S(2)}, u32[]{:S(2)}) collective-permute-start(bf16[256,512]{1,0:T(8,128)(2,1)} %collective-permute-done.16), channel_id=1, source_target_pairs={{0,192},{1,193},{2,194},{3,195},{4,196},{5,197},{6,198},{7,199},{8... | collective-permute-start | bytes 786440 | tf_op jit(solution)/shard_map/cond/branch_2_fun/ppermute | solution.py:59
  18.3 67.0 %collective-permute-start.20 = (bf16[256,512]{1,0:T(8,128)(2,1)}, bf16[256,512]{1,0:T(8,128)(2,1)S(1)}, u32[]{:S(2)}, u32[]{:S(2)}) collective-permute-start(bf16[256,512]{1,0:T(8,128)(2,1)} %collective-permute-done.19), channel_id=1, source_target_pairs={{0,192},{1,193},{2,194},{3,195},{4,196},{5,197},{6,198},{7,199},{8... | collective-permute-start | bytes 786440 | tf_op jit(solution)/shard_map/cond/branch_2_fun/ppermute | solution.py:59
  39.3 45.5 %copy-start.7 = (bf16[512,512]{1,0:T(8,128)(2,1)S(1)}, bf16[512,512]{1,0:T(8,128)(2,1)}, u32[]{:S(2)}) copy-start(bf16[512,512]{1,0:T(8,128)(2,1)} %get-tuple-element.88) | copy-start | bytes 1572868 | tf_op jit(solution)/shard_map/cond
  39.8 45.6 %slice-start.1 = ((f32[512,1024]{1,0:T(8,128)}), f32[256,1024]{1,0:T(8,128)S(1)}, s32[]{:S(2)}) async-start(f32[512,1024]{1,0:T(8,128)} %fusion.112), calls=%async_computation.1 | async-start | bytes 2097152 | tf_op jit(solution)/shard_map/cond/branch_2_fun/slice | solution.py:93
  39.8 83.4 %collective-permute-start.22 = (bf16[256,512]{1,0:T(8,128)(2,1)S(1)}, bf16[256,512]{1,0:T(8,128)(2,1)S(1)}, u32[]{:S(2)}, u32[]{:S(2)}) collective-permute-start(bf16[256,512]{1,0:T(8,128)(2,1)S(1)} %fusion.108), channel_id=1, source_target_pairs={{128,64},{129,65},{130,66},{131,67},{132,68},{133,69},{134,70},{13... | collective-permute-start | bytes 786440 | tf_op jit(solution)/shard_map/cond/branch_2_fun/ppermute | solution.py:59
  86.7 36.1 %copy-start.20 = (bf16[512,512]{1,0:T(8,128)(2,1)S(1)}, bf16[512,512]{1,0:T(8,128)(2,1)}, u32[]{:S(2)}) copy-start(bf16[512,512]{1,0:T(8,128)(2,1)} %get-tuple-element.94) | copy-start | bytes 1572868 | tf_op jit(solution)/shard_map/cond
  86.7 36.1 %collective-permute-start.23 = (bf16[256,512]{1,0:T(8,128)(2,1)S(1)}, bf16[256,512]{1,0:T(8,128)(2,1)S(1)}, u32[]{:S(2)}, u32[]{:S(2)}) collective-permute-start(bf16[256,512]{1,0:T(8,128)(2,1)S(1)} %fusion.109), channel_id=1, source_target_pairs={{128,64},{129,65},{130,66},{131,67},{132,68},{133,69},{134,70},{13... | collective-permute-start | bytes 786440 | tf_op jit(solution)/shard_map/cond/branch_2_fun/ppermute | solution.py:59

commit v3 on v2

v3 whole, which is shorter than its diff:
```python
import functools

import jax
import jax.numpy as jnp
from jax import lax
from jax.experimental import pallas as pl
from jax.experimental.pallas import tpu as pltpu
from jax.sharding import PartitionSpec as P


BLOCKS = 8
CONTRACT = (((1,), (1,)), ((), ()))


class Route:
    def __init__(self, edges, forward, backward):
        self.edges, self.forward, self.backward = edges, forward, backward


def plain(edges):
    forward = tuple((i, i + 1) for i in edges)
    backward = tuple((i + 1, i) for i in edges)
    return Route(tuple(edges), (forward, ()), (backward, ()))


def routed(forward, forward_splits, backward, backward_splits):
    edges = [a for a, _ in forward] + [a for a, _, _ in forward_splits]
    assert sorted(edges) == sorted([b for _, b in backward] + [b for _, _, b in backward_splits])
    return Route(tuple(edges), (forward, forward_splits), (backward, backward_splits))


ROUTES = (
    routed(
        ((2, 3), (4, 5)),
        ((0, 6, 1), (3, 7, 4)),
        ((1, 0), (5, 4)),
        ((3, 7, 2), (4, 6, 3)),
    ),
    routed(
        ((1, 2), (5, 6)),
        ((2, 0, 3), (3, 7, 4)),
        ((2, 1), (6, 5)),
        ((3, 7, 2), (4, 0, 3)),
    ),
    routed(
        ((1, 2), (6, 7)),
        ((2, 0, 3), (3, 5, 4)),
        ((2, 1), (7, 6)),
        ((3, 5, 2), (4, 0, 3)),
    ),
    plain((0, 2, 3, 4, 6)),
    plain(range(BLOCKS - 1)),
)


def route_kernel(gap, rows, me_ref, lengths_ref, out_ref):
    position = lax.rem(me_ref[0], gap)
    reach = gap * rows
    starts = [lengths_ref[0]]
    for k in range(1, lengths_ref.shape[0] - 1):
        starts.append(starts[-1] + lengths_ref[k])
    total = starts[-1] + lengths_ref[lengths_ref.shape[0] - 1]
    live = []
    for edge in range(BLOCKS - 1):
        first = ((edge + 1) * gap + position) * rows
        dead = first >= total
        for start in starts:
            dead = dead | ((start <= first) & (first + rows <= start + reach))
        live.append(jnp.logical_not(dead))
    choice = jnp.int32(len(ROUTES) - 1)
    for k in reversed(range(len(ROUTES) - 1)):
        missed = jnp.bool_(False)
        for edge in range(BLOCKS - 1):
            if edge not in ROUTES[k].edges:
                missed = missed | live[edge]
        choice = jnp.where(missed, choice, jnp.int32(k))
    out_ref[0] = choice


def choose_route(me, lengths, gap, rows):
    smem = pl.BlockSpec(memory_space=pltpu.SMEM)
    return pl.pallas_call(
        functools.partial(route_kernel, gap, rows),
        out_shape=jax.ShapeDtypeStruct((1,), jnp.int32),
        in_specs=[smem, smem],
        out_specs=smem,
        name="route",
    )(me.reshape(1), lengths)[0]


def move(value, gap, pairs):
    return lax.ppermute(
        value, "tm", [(a * gap + r, b * gap + r) for a, b in pairs for r in range(gap)]
    )


def among(block, blocks):
    found = block == blocks[0]
    for b in blocks[1:]:
        found = found | (block == b)
    return found


def exchange(first, second, gap, block, plan):
    sends, splits = plan
    if splits:
        held = move(second, gap, [(a, relay) for a, relay, _ in splits])
    first = move(first, gap, sends + tuple((a, b) for a, _, b in splits))
    second = move(second, gap, sends)
    if splits:
        passed = move(held, gap, [(relay, b) for _, relay, b in splits])
        second = jnp.where(among(block, [b for _, _, b in splits]), passed, second)
    return first, second


def layer(route, trace, me, lengths, conv_weight, res_weight, cotangent):
    row_count = trace.shape[0]
    half = row_count // 2
    gap = lax.axis_size("tm") // BLOCKS
    block = lax.div(me, jnp.int32(gap))
    half_width = conv_weight.shape[2] // 2

    past = exchange(trace[:half], trace[half:], gap, block, route.forward)

    positions = me * row_count + lax.broadcasted_iota(jnp.int32, (row_count, 1), 0)
    ends = jnp.cumsum(lengths)
    starts = ends - lengths
    begin = jnp.max(jnp.where(starts[None, :] <= positions, starts[None, :], 0), axis=1, keepdims=True)
    inside = positions < jnp.sum(lengths)
    tap = inside & (positions - row_count * gap >= begin)
    valid_f = inside.astype(jnp.float32)

    delayed = jnp.where(tap, jnp.concatenate(past, axis=0), jnp.bfloat16(0))
    taps = jnp.concatenate([delayed, trace], axis=1)
    preact = jnp.dot(
        taps, conv_weight.reshape(-1, conv_weight.shape[2]), preferred_element_type=jnp.float32
    )
    filt_tanh = jnp.tanh(preact[:, :half_width])
    gate_sig = jax.nn.sigmoid(preact[:, half_width:])
    mixed = (filt_tanh * gate_sig * valid_f).astype(jnp.bfloat16)
    mix = lax.dot_general(cotangent, res_weight, CONTRACT, preferred_element_type=jnp.float32)
    grad_mix = mix * valid_f
    grad_filt = grad_mix * gate_sig * (1.0 - filt_tanh * filt_tanh)
    grad_gate = grad_mix * filt_tanh * gate_sig * (1.0 - gate_sig)
    grad_pre = jnp.concatenate([grad_filt, grad_gate], axis=1).astype(jnp.bfloat16)

    def own(rows):
        value = lax.dot_general(
            grad_pre[rows], conv_weight[0], CONTRACT, preferred_element_type=jnp.float32
        )
        return jnp.where(tap[rows], value, 0.0).astype(jnp.bfloat16)

    own_first, own_second = own(slice(0, half)), own(slice(half, row_count))
    partial = exchange(own_first, own_second, gap, block, route.backward)
    output = (
        trace.astype(jnp.float32) + jnp.dot(mixed, res_weight, preferred_element_type=jnp.float32)
    ).astype(jnp.bfloat16)
    local = cotangent.astype(jnp.float32) + lax.dot_general(
        grad_pre, conv_weight[1], CONTRACT, preferred_element_type=jnp.float32
    )
    local = lax.optimization_barrier(local)
    partial = jnp.concatenate(partial, axis=0).astype(jnp.float32)
    return (output, (local + partial).astype(jnp.bfloat16))


def per_device(trace, lengths, conv_weight, res_weight, cotangent):
    gap = lax.axis_size("tm") // BLOCKS
    me = lax.axis_index("tm")
    choice = choose_route(me, lengths, gap, trace.shape[0])
    branches = [functools.partial(layer, route) for route in ROUTES]
    return lax.switch(choice, branches, trace, me, lengths, conv_weight, res_weight, cotangent)


def solution(mesh):
    in_specs = (P("tm", None), P(), P(), P(), P("tm", None))
    out_specs = (P("tm", None), P("tm", None))
    return jax.shard_map(
        per_device, mesh=mesh, in_specs=in_specs, out_specs=out_specs, check_vma=False
    )
```

time: 126 us -> 116 us (0.921)
  the two profiles are of different devices: /device:TPU:53 before, /device:TPU:107 now
where the time goes in v3:
time: 116 us
  waiting for transfers between devices  75.8 us (65%)
  starting transfers between devices  23.2 us (20%)
  matrix products  6.96 us (6%)
  other arithmetic  5.41 us (5%)
  local copies, waits for them, and re-layouts  1.9 us (2%)
  between operations  1.29 us (1%)
  Pallas kernels  1.22 us (1%)
    ppermute x8, waiting for transfers between devices, move(): lax.ppermute(value, 'tm', [(a * gap + r, b * gap + r) for a, b in pairs f...  75.8 us
    ppermute x8, starting transfers between devices, move(): lax.ppermute(value, 'tm', [(a * gap + r, b * gap + r) for a, b in pairs f...  23.2 us
    dot_general x1, matrix products, layer(): jnp.dot(taps, conv_weight.reshape(-1, conv_weight.shape[2]), preferred_el...  2.93 us
  transfers between devices with their start and end apart: 8, of which 4 were waited for; matrix products, arithmetic and copies ran while one was open for 6% of the time, Pallas kernels for 0%

profile of v3, /device:TPU:107, one launch (start us, length us, event | category | flops | bytes accessed | tf_op | source)
XLA Modules:
  0.0 116.0 jit_solution(14322378541029174366)
XLA Ops:
  0.6 1.2 %route.1 = s32[1]{0:T(128)} custom-call(s32[1]{0:T(128)} %bitcast.30.me_ref, s32[4]{0:T(128)} %lengths_ref.1), custom_call_target="tpu_custom_call" | custom-call | tf_op jit(solution)/shard_map/route/pallas_call | solution.py:82
  2.5 113.5 %conditional.4 = (bf16[512,512]{1,0:T(8,128)(2,1)}, bf16[512,512]{1,0:T(8,128)(2,1)}) conditional(s32[]{:T(128)} %bitcast.31, (bf16[512,512]{1,0:T(8,128)(2,1)}, s32[]{:T(128)}, s32[4]{0:T(128)}, bf16[2,512,1024]{2,1,0:T(8,128)(2,1)}, bf16[512,512]{1,0:T(8,128)(2,1)}, ...), branch_computations={%region_0.4_spmd, %region_4.8_spmd, %region_8.12_spmd, %region_12.... | conditional | flops 2700882432 | bytes 50352312
  2.5 0.0 copy-start.1
  2.5 1.1 fusion.142
  3.7 1.3 %collective-permute-start.11 = (bf16[256,512]{1,0:T(8,128)(2,1)S(1)}, bf16[256,512]{1,0:T(8,128)(2,1)S(1)}, u32[]{:S(2)}, u32[]{:S(2)}) collective-permute-start(bf16[256,512]{1,0:T(8,128)(2,1)S(1)} %get-tuple-element.129), channel_id=1, source_target_pairs={{64,128},{65,129},{66,130},{67,131},{68,132},{69,133},{70,134},{71... | collective-permute-start | bytes 786440 | tf_op jit(solution)/shard_map/cond/branch_1_fun/ppermute | solution.py:92
  5.0 1.5 %collective-permute-start.9 = (bf16[256,512]{1,0:T(8,128)(2,1)S(1)}, bf16[256,512]{1,0:T(8,128)(2,1)S(1)}, u32[]{:S(2)}, u32[]{:S(2)}) collective-permute-start(bf16[256,512]{1,0:T(8,128)(2,1)S(1)} %get-tuple-element.129), channel_id=1, source_target_pairs={{128,0},{129,1},{130,2},{131,3},{132,4},{133,5},{134,6},{135,7},{1... | collective-permute-start | bytes 786440 | tf_op jit(solution)/shard_map/cond/branch_1_fun/ppermute | solution.py:92
  6.5 14.6 %collective-permute-start.8 = (bf16[256,512]{1,0:T(8,128)(2,1)S(1)}, bf16[256,512]{1,0:T(8,128)(2,1)S(1)}, u32[]{:S(2)}, u32[]{:S(2)}) collective-permute-start(bf16[256,512]{1,0:T(8,128)(2,1)S(1)} %get-tuple-element.128), channel_id=1, source_target_pairs={{64,128},{65,129},{66,130},{67,131},{68,132},{69,133},{70,134},{71... | collective-permute-start | bytes 786440 | tf_op jit(solution)/shard_map/cond/branch_1_fun/ppermute | solution.py:92
  21.1 0.8 reduce-window.41
  21.9 1.3 %fusion.143 = (s32[]{:T(128)}, s32[4]{0:T(128)S(1)}) fusion(s32[4]{0:T(128)} %get-tuple-element.80, s32[4,1]{0,1:T(1,128)S(1)} %reduce-window.41), kind=kLoop, calls=%fused_computation.254 | loop fusion | flops 7 | bytes 52 | tf_op jit(solution)/shard_map/cond/branch_1_fun/reduce_sum | solution.py:129
  23.2 0.1 select_reduce_fusion.1
  23.3 0.7 compare_and_fusion.1
  23.9 0.0 collective-permute-done.9
  23.9 0.7 collective-permute-start.10
  24.6 0.7 fusion.48
  25.3 0.7 fusion.50
  26.0 13.0 %collective-permute-done.11 = bf16[256,512]{1,0:T(8,128)(2,1)S(1)} collective-permute-done((bf16[256,512]{1,0:T(8,128)(2,1)S(1)}, bf16[256,512]{1,0:T(8,128)(2,1)S(1)}, u32[]{:S(2)}, u32[]{:S(2)}) %collective-permute-start.11) | collective-permute-done | bytes 262176 | tf_op jit(solution)/shard_map/cond/branch_1_fun/ppermute | solution.py:92
  39.0 0.0 collective-permute-done.10
  39.0 21.1 %collective-permute-done.8 = bf16[256,512]{1,0:T(8,128)(2,1)S(1)} collective-permute-done((bf16[256,512]{1,0:T(8,128)(2,1)S(1)}, bf16[256,512]{1,0:T(8,128)(2,1)S(1)}, u32[]{:S(2)}, u32[]{:S(2)}) %collective-permute-start.8) | collective-permute-done | bytes 262176 | tf_op jit(solution)/shard_map/cond/branch_1_fun/ppermute | solution.py:92
  60.1 0.2 maximum_select_fusion.1
  60.3 0.0 copy-done.1
  60.3 0.0 copy-start.11
  60.3 0.0 copy-start.16
  60.3 2.9 %fusion.33 = f32[512,1024]{1,0:T(8,128)S(1)} fusion(bf16[1024,1024]{1,0:T(8,128)(2,1)} %bitcast.98, bf16[512,512]{1,0:T(8,128)(2,1)S(1)} %copy-done.1, bf16[512,512]{1,0:T(8,128)(2,1)S(1)} %maximum_select_fusion.1), kind=kOutput, calls=%fused_computation.68 | convolution fusion | flops 1075838976 | bytes 5242880 | tf_op jit(solution)/shard_map/cond/branch_1_fun/dot_general | solution.py:135
  63.3 0.0 copy-done.11
  63.3 0.0 copy-done.16
  63.3 0.0 copy-start.6
  63.3 0.8 multiply_convert_fusion.5
  64.1 0.7 copy-done.6
  64.9 0.5 fusion.29
  65.3 1.3 %collective-permute-start.15 = (bf16[256,512]{1,0:T(8,128)(2,1)S(1)}, bf16[256,512]{1,0:T(8,128)(2,1)S(1)}, u32[]{:S(2)}, u32[]{:S(2)}) collective-permute-start(bf16[256,512]{1,0:T(8,128)(2,1)S(1)} %fusion.29), channel_id=1, source_target_pairs={{128,64},{129,65},{130,66},{131,67},{132,68},{133,69},{134,70},{13... | collective-permute-start | bytes 786440 | tf_op jit(solution)/shard_map/cond/branch_1_fun/ppermute | solution.py:92
  66.7 0.7 collective-permute-start.13
  67.3 0.5 fusion.28
  67.8 1.9 %collective-permute-start.12 = (bf16[256,512]{1,0:T(8,128)(2,1)S(1)}, bf16[256,512]{1,0:T(8,128)(2,1)S(1)}, u32[]{:S(2)}, u32[]{:S(2)}) collective-permute-start(bf16[256,512]{1,0:T(8,128)(2,1)S(1)} %fusion.28), channel_id=1, source_target_pairs={{128,64},{129,65},{130,66},{131,67},{132,68},{133,69},{134,70},{13... | collective-permute-start | bytes 786440 | tf_op jit(solution)/shard_map/cond/branch_1_fun/ppermute | solution.py:92
  69.8 1.5 %convolution_add_fusion.3 = bf16[512,512]{1,0:T(8,128)(2,1)} fusion(bf16[512,512]{1,0:T(8,128)(2,1)S(1)} %copy-done.11, bf16[512,512]{1,0:T(8,128)(2,1)S(1)} %copy-done.1, f32[512,1024]{1,0:T(8,128)S(1)} %fusion.33, f32[512]{0:T(512)S(1)} %fusion.50), kind=kOutput, calls=%fused_computation.53 | convolution fusion | flops 270794752 | bytes 3672064 | tf_op jit(solution)/shard_map/cond/branch_1_fun/dot_general | solution.py:156
  71.3 0.0 collective-permute-done.13
  71.3 1.3 %collective-permute-start.14 = (bf16[256,512]{1,0:T(8,128)(2,1)S(1)}, bf16[256,512]{1,0:T(8,128)(2,1)S(1)}, u32[]{:S(2)}, u32[]{:S(2)}) collective-permute-start(bf16[256,512]{1,0:T(8,128)(2,1)S(1)} %collective-permute-done.13), channel_id=1, source_target_pairs={{448,128},{449,129},{450,130},{451,131},{452,132},{453,133},{454,1... | collective-permute-start | bytes 786440 | tf_op jit(solution)/shard_map/cond/branch_1_fun/ppermute | solution.py:92
  72.5 0.7 convolution_add_fusion.2
  73.3 9.3 %collective-permute-done.15 = bf16[256,512]{1,0:T(8,128)(2,1)S(1)} collective-permute-done((bf16[256,512]{1,0:T(8,128)(2,1)S(1)}, bf16[256,512]{1,0:T(8,128)(2,1)S(1)}, u32[]{:S(2)}, u32[]{:S(2)}) %collective-permute-start.15) | collective-permute-done | bytes 262176 | tf_op jit(solution)/shard_map/cond/branch_1_fun/ppermute | solution.py:92
  82.6 32.4 %collective-permute-done.14 = bf16[256,512]{1,0:T(8,128)(2,1)S(1)} collective-permute-done((bf16[256,512]{1,0:T(8,128)(2,1)S(1)}, bf16[256,512]{1,0:T(8,128)(2,1)S(1)}, u32[]{:S(2)}, u32[]{:S(2)}) %collective-permute-start.14) | collective-permute-done | bytes 262176 | tf_op jit(solution)/shard_map/cond/branch_1_fun/ppermute | solution.py:92
  115.0 0.0 collective-permute-done.12
  115.0 1.0 convert_add_fusion.1
  (4 shorter events, 0.1 us)
Async XLA Ops:
  2.5 57.8 %copy-start.1 = (bf16[512,512]{1,0:T(8,128)(2,1)S(1)}, bf16[512,512]{1,0:T(8,128)(2,1)}, u32[]{:S(2)}) copy-start(bf16[512,512]{1,0:T(8,128)(2,1)} %get-tuple-element.78) | copy-start | bytes 1572868
  3.7 35.3 %collective-permute-start.11 = (bf16[256,512]{1,0:T(8,128)(2,1)S(1)}, bf16[256,512]{1,0:T(8,128)(2,1)S(1)}, u32[]{:S(2)}, u32[]{:S(2)}) collective-permute-start(bf16[256,512]{1,0:T(8,128)(2,1)S(1)} %get-tuple-element.129), channel_id=1, source_target_pairs={{64,128},{65,129},{66,130},{67,131},{68,132},{69,133},{70,134},{71... | collective-permute-start | bytes 786440 | tf_op jit(solution)/shard_map/cond/branch_1_fun/ppermute | solution.py:92
  5.0 19.0 %collective-permute-start.9 = (bf16[256,512]{1,0:T(8,128)(2,1)S(1)}, bf16[256,512]{1,0:T(8,128)(2,1)S(1)}, u32[]{:S(2)}, u32[]{:S(2)}) collective-permute-start(bf16[256,512]{1,0:T(8,128)(2,1)S(1)} %get-tuple-element.129), channel_id=1, source_target_pairs={{128,0},{129,1},{130,2},{131,3},{132,4},{133,5},{134,6},{135,7},{1... | collective-permute-start | bytes 786440 | tf_op jit(solution)/shard_map/cond/branch_1_fun/ppermute | solution.py:92
  6.5 53.6 %collective-permute-start.8 = (bf16[256,512]{1,0:T(8,128)(2,1)S(1)}, bf16[256,512]{1,0:T(8,128)(2,1)S(1)}, u32[]{:S(2)}, u32[]{:S(2)}) collective-permute-start(bf16[256,512]{1,0:T(8,128)(2,1)S(1)} %get-tuple-element.128), channel_id=1, source_target_pairs={{64,128},{65,129},{66,130},{67,131},{68,132},{69,133},{70,134},{71... | collective-permute-start | bytes 786440 | tf_op jit(solution)/shard_map/cond/branch_1_fun/ppermute | solution.py:92
  23.9 15.0 %collective-permute-start.10 = (bf16[256,512]{1,0:T(8,128)(2,1)S(1)}, bf16[256,512]{1,0:T(8,128)(2,1)S(1)}, u32[]{:S(2)}, u32[]{:S(2)}) collective-permute-start(bf16[256,512]{1,0:T(8,128)(2,1)S(1)} %collective-permute-done.9), channel_id=1, source_target_pairs={{0,192},{1,193},{2,194},{3,195},{4,196},{5,197},{6,198},{7,199},{8... | collective-permute-start | bytes 786440 | tf_op jit(solution)/shard_map/cond/branch_1_fun/ppermute | solution.py:92
  60.3 3.0 %copy-start.11 = (bf16[512,512]{1,0:T(8,128)(2,1)S(1)}, bf16[512,512]{1,0:T(8,128)(2,1)}, u32[]{:S(2)}) copy-start(bf16[512,512]{1,0:T(8,128)(2,1)} %get-tuple-element.82) | copy-start | bytes 1572868
  60.3 3.0 %copy-start.16 = (bf16[512,512]{1,0:T(8,128)(2,1)S(1)}, bf16[512,512]{1,0:T(8,128)(2,1)}, u32[]{:S(2)}) copy-start(bf16[512,512]{1,0:T(8,128)(2,1)} %get-tuple-element.83) | copy-start | bytes 1572868
  63.3 1.6 %copy-start.6 = (bf16[2,512,1024]{2,1,0:T(8,128)(2,1)S(1)}, bf16[2,512,1024]{2,1,0:T(8,128)(2,1)}, u32[]{:S(2)}) copy-start(bf16[2,512,1024]{2,1,0:T(8,128)(2,1)} %get-tuple-element.81) | copy-start | bytes 6291460
  65.3 17.3 %collective-permute-start.15 = (bf16[256,512]{1,0:T(8,128)(2,1)S(1)}, bf16[256,512]{1,0:T(8,128)(2,1)S(1)}, u32[]{:S(2)}, u32[]{:S(2)}) collective-permute-start(bf16[256,512]{1,0:T(8,128)(2,1)S(1)} %fusion.29), channel_id=1, source_target_pairs={{128,64},{129,65},{130,66},{131,67},{132,68},{133,69},{134,70},{13... | collective-permute-start | bytes 786440 | tf_op jit(solution)/shard_map/cond/branch_1_fun/ppermute | solution.py:92
  66.7 4.6 %collective-permute-start.13 = (bf16[256,512]{1,0:T(8,128)(2,1)S(1)}, bf16[256,512]{1,0:T(8,128)(2,1)S(1)}, u32[]{:S(2)}, u32[]{:S(2)}) collective-permute-start(bf16[256,512]{1,0:T(8,128)(2,1)S(1)} %fusion.29), channel_id=1, source_target_pairs={{192,448},{193,449},{194,450},{195,451},{196,452},{197,453},{198,4... | collective-permute-start | bytes 786440 | tf_op jit(solution)/shard_map/cond/branch_1_fun/ppermute | solution.py:92
  67.8 47.2 %collective-permute-start.12 = (bf16[256,512]{1,0:T(8,128)(2,1)S(1)}, bf16[256,512]{1,0:T(8,128)(2,1)S(1)}, u32[]{:S(2)}, u32[]{:S(2)}) collective-permute-start(bf16[256,512]{1,0:T(8,128)(2,1)S(1)} %fusion.28), channel_id=1, source_target_pairs={{128,64},{129,65},{130,66},{131,67},{132,68},{133,69},{134,70},{13... | collective-permute-start | bytes 786440 | tf_op jit(solution)/shard_map/cond/branch_1_fun/ppermute | solution.py:92
  71.3 43.7 %collective-permute-start.14 = (bf16[256,512]{1,0:T(8,128)(2,1)S(1)}, bf16[256,512]{1,0:T(8,128)(2,1)S(1)}, u32[]{:S(2)}, u32[]{:S(2)}) collective-permute-start(bf16[256,512]{1,0:T(8,128)(2,1)S(1)} %collective-permute-done.13), channel_id=1, source_target_pairs={{448,128},{449,129},{450,130},{451,131},{452,132},{453,133},{454,1... | collective-permute-start | bytes 786440 | tf_op jit(solution)/shard_map/cond/branch_1_fun/ppermute | solution.py:92

commit v4 on v3

--- a/solution.py
+++ b/solution.py
@@ -11,6 +11,9 @@
 BLOCKS = 8
 CONTRACT = (((1,), (1,)), ((), ()))
 
+VARIANTS = 3
+SLICES = 4
+
 
 class Route:
     def __init__(self, edges, forward, backward):
@@ -18,35 +21,46 @@
 
 
 def plain(edges):
-    forward = tuple((i, i + 1) for i in edges)
-    backward = tuple((i + 1, i) for i in edges)
-    return Route(tuple(edges), (forward, ()), (backward, ()))
-
-
-def routed(forward, forward_splits, backward, backward_splits):
-    edges = [a for a, _ in forward] + [a for a, _, _ in forward_splits]
-    assert sorted(edges) == sorted([b for _, b in backward] + [b for _, _, b in backward_splits])
-    return Route(tuple(edges), (forward, forward_splits), (backward, backward_splits))
+    forward = ((tuple((i, i + 1) for i in edges), ()),)
+    backward = tuple(
+        (tuple((i + 1, i) for i in edges if i % 2 == odd), ()) for odd in range(2)
+    )
+    return Route(tuple(edges), (forward,) * VARIANTS, (backward,) * VARIANTS)
+
+
+def group(sends, relays):
+    return (
+        tuple((a, b) for a, b in sends if a not in relays),
+        tuple((a, relays[a], b) for a, b in sends if a in relays),
+    )
+
+
+def routed(many, lone, relays, back_relays):
+    forward = [(group([(i, i + 1) for i in sorted(many + lone)], r),) for r in relays]
+    backward = [
+        tuple(group([(i + 1, i) for i in edges], r) for edges in (many, lone)) for r in back_relays
+    ]
+    return Route(many + lone, forward, backward)
 
 
 ROUTES = (
     routed(
-        ((2, 3), (4, 5)),
-        ((0, 6, 1), (3, 7, 4)),
-        ((1, 0), (5, 4)),
-        ((3, 7, 2), (4, 6, 3)),
+        (0, 2, 4),
+        (3,),
+        [{a: 6, 3: 7} for a in (0, 2, 4)],
+        [{a: 7, 4: 6} for a in (1, 3, 5)],
     ),
     routed(
-        ((1, 2), (5, 6)),
-        ((2, 0, 3), (3, 7, 4)),
-        ((2, 1), (6, 5)),
-        ((3, 7, 2), (4, 0, 3)),
+        (1, 3, 5),
+        (2,),
+        [{a: 7, 2: 0} for a in (1, 3, 5)],
+        [{a: 0, 3: 7} for a in (2, 4, 6)],
     ),
     routed(
-        ((1, 2), (6, 7)),
-        ((2, 0, 3), (3, 5, 4)),
-        ((2, 1), (7, 6)),
-        ((3, 5, 2), (4, 0, 3)),
+        (1, 3),
+        (2, 6),
+        [{a: 5, 2: 0} for a in (1, 3, 1)],
+        [{a: 0, 3: 5} for a in (4, 2, 4)],
     ),
     plain((0, 2, 3, 4, 6)),
     plain(range(BLOCKS - 1)),
@@ -89,28 +103,49 @@
 
 
 def move(value, gap, pairs):
+    width = gap // SLICES
     return lax.ppermute(
-        value, "tm", [(a * gap + r, b * gap + r) for a, b in pairs for r in range(gap)]
-    )
-
-
-def among(block, blocks):
-    found = block == blocks[0]
-    for b in blocks[1:]:
-        found = found | (block == b)
+        value,
+        "tm",
+        [
+            (a * gap + r, b * gap + r)
+            for r in range(gap)
+            for a, b in pairs[(r // width) % VARIANTS]
+        ],
+    )
+
+
+def among(place, blocks):
+    block, variant = place
+    if all(set(b) == set(blocks[0]) for b in blocks):
+        blocks, variant = blocks[:1], None
+    found = jnp.bool_(False)
+    for v, names in enumerate(blocks):
+        here = jnp.bool_(False)
+        for b in names:
+            here = here | (block == b)
+        found = found | (here if variant is None else here & (variant == v))
     return found
 
 
-def exchange(first, second, gap, block, plan):
-    sends, splits = plan
-    if splits:
-        held = move(second, gap, [(a, relay) for a, relay, _ in splits])
-    first = move(first, gap, sends + tuple((a, b) for a, _, b in splits))
-    second = move(second, gap, sends)
-    if splits:
-        passed = move(held, gap, [(relay, b) for _, relay, b in splits])
-        second = jnp.where(among(block, [b for _, _, b in splits]), passed, second)
-    return first, second
+def exchange(first, second, gap, place, plans):
+    splits = [[split for group in plan for split in group[1]] for plan in plans]
+    if splits[0]:
+        held = move(second, gap, [[(a, relay) for a, relay, _ in s] for s in splits])
+    near = next_ = None
+    for k in range(len(plans[0])):
+        sends = [plan[k][0] for plan in plans]
+        direct = [plan[k][0] + tuple((a, b) for a, _, b in plan[k][1]) for plan in plans]
+        arrived = move(first, gap, direct)
+        here = among(place, [[b for _, b in d] for d in direct])
+        near = arrived if near is None else jnp.where(here, arrived, near)
+        if sends[0]:
+            arrived = move(second, gap, sends)
+            next_ = arrived if next_ is None else jnp.where(here, arrived, next_)
+    if splits[0]:
+        passed = move(held, gap, [[(relay, b) for _, relay, b in s] for s in splits])
+        next_ = jnp.where(among(place, [[b for _, _, b in s] for s in splits]), passed, next_)
+    return near, next_
 
 
 def layer(route, trace, me, lengths, conv_weight, res_weight, cotangent):
@@ -118,9 +153,12 @@
     half = row_count // 2
     gap = lax.axis_size("tm") // BLOCKS
     block = lax.div(me, jnp.int32(gap))
+    variant = lax.rem(lax.div(lax.rem(me, jnp.int32(gap)), jnp.int32(gap // SLICES)), jnp.int32(VARIANTS))
+    place = (block, variant)
     half_width = conv_weight.shape[2] // 2
 
-    past = exchange(trace[:half], trace[half:], gap, block, route.forward)
+    past = exchange(trace[:half], trace[half:], gap, place, route.forward)
+    here = jnp.dot(trace, conv_weight[1], preferred_element_type=jnp.float32)
 
     positions = me * row_count + lax.broadcasted_iota(jnp.int32, (row_count, 1), 0)
     ends = jnp.cumsum(lengths)
@@ -131,10 +169,8 @@
     valid_f = inside.astype(jnp.float32)
 
     delayed = jnp.where(tap, jnp.concatenate(past, axis=0), jnp.bfloat16(0))
-    taps = jnp.concatenate([delayed, trace], axis=1)
-    preact = jnp.dot(
-        taps, conv_weight.reshape(-1, conv_weight.shape[2]), preferred_element_type=jnp.float32
-    )
+    delayed = lax.optimization_barrier(delayed)
+    preact = jnp.dot(delayed, conv_weight[0], preferred_element_type=jnp.float32) + here
     filt_tanh = jnp.tanh(preact[:, :half_width])
     gate_sig = jax.nn.sigmoid(preact[:, half_width:])
     mixed = (filt_tanh * gate_sig * valid_f).astype(jnp.bfloat16)
@@ -151,7 +187,7 @@
         return jnp.where(tap[rows], value, 0.0).astype(jnp.bfloat16)
 
     own_first, own_second = own(slice(0, half)), own(slice(half, row_count))
-    partial = exchange(own_first, own_second, gap, block, route.backward)
+    partial = exchange(own_first, own_second, gap, place, route.backward)
     output = (
         trace.astype(jnp.float32) + jnp.dot(mixed, res_weight, preferred_element_type=jnp.float32)
     ).astype(jnp.bfloat16)

time: 116 us -> 109 us (0.940)
  the two profiles are of different devices: /device:TPU:107 before, /device:TPU:15 now
where the time goes in v4:
time: 109 us
  waiting for transfers between devices  63.4 us (58%)
  starting transfers between devices  26.2 us (24%)
  matrix products  10.1 us (9%)
  other arithmetic  5.43 us (5%)
  between operations  1.29 us (1%)
  Pallas kernels  1.22 us (1%)
  local copies, waits for them, and re-layouts  1.11 us (1%)
    ppermute x9, waiting for transfers between devices, move(): lax.ppermute(value, 'tm', [(a * gap + r, b * gap + r) for r in range(gap)...  63.4 us
    ppermute x9, starting transfers between devices, move(): lax.ppermute(value, 'tm', [(a * gap + r, b * gap + r) for r in range(gap)...  26.2 us
    dot_general x1, matrix products, layer(): here = jnp.dot(trace, conv_weight[1], preferred_element_type=jnp.float32)  3.6 us
    dot_general x1, matrix products, layer(): jnp.dot(delayed, conv_weight[0], preferred_element_type=jnp.float32) + here  2.43 us
  transfers between devices with their start and end apart: 9, of which 3 were waited for; matrix products, arithmetic and copies ran while one was open for 10% of the time, Pallas kernels for 0%

profile of v4, /device:TPU:15, one launch (start us, length us, event | category | flops | bytes accessed | tf_op | source)
XLA Modules:
  0.0 109.1 jit_solution(4524897809760567503)
XLA Ops:
  0.6 1.2 %route.1 = s32[1]{0:T(128)} custom-call(s32[1]{0:T(128)} %bitcast.25.me_ref, s32[4]{0:T(128)} %lengths_ref.1), custom_call_target="tpu_custom_call" | custom-call | tf_op jit(solution)/shard_map/route/pallas_call | solution.py:96
  2.5 106.6 %conditional.4 = (bf16[512,512]{1,0:T(8,128)(2,1)}, bf16[512,512]{1,0:T(8,128)(2,1)}) conditional(s32[]{:T(128)} %bitcast.26, (bf16[512,512]{1,0:T(8,128)(2,1)}, s32[]{:T(128)}, s32[4]{0:T(128)}, bf16[2,512,1024]{2,1,0:T(8,128)(2,1)}, bf16[512,512]{1,0:T(8,128)(2,1)}, ...), branch_computations={%region_0.4_spmd, %region_4.8_spmd, %region_8.12_spmd, %region_12.... | conditional | flops 2699571712 | bytes 57692608
  2.5 1.1 fusion.140
  3.6 15.5 %collective-permute-start.3 = (bf16[256,512]{1,0:T(8,128)(2,1)S(1)}, bf16[256,512]{1,0:T(8,128)(2,1)S(1)}, u32[]{:S(2)}, u32[]{:S(2)}) collective-permute-start(bf16[256,512]{1,0:T(8,128)(2,1)S(1)} %get-tuple-element.123), channel_id=1, source_target_pairs={{128,192},{256,320},{129,193},{257,321},{130,194},{258,322},{131,1... | collective-permute-start | bytes 786440 | tf_op jit(solution)/shard_map/cond/branch_0_fun/ppermute | solution.py:107
  19.1 1.4 %collective-permute-start.1 = (bf16[256,512]{1,0:T(8,128)(2,1)S(1)}, bf16[256,512]{1,0:T(8,128)(2,1)}, u32[]{:S(2)}, u32[]{:S(2)}) collective-permute-start(bf16[256,512]{1,0:T(8,128)(2,1)S(1)} %get-tuple-element.123), channel_id=1, source_target_pairs={{0,384},{192,448},{1,385},{193,449},{2,386},{194,450},{3,387},{195... | collective-permute-start | bytes 786440 | tf_op jit(solution)/shard_map/cond/branch_0_fun/ppermute | solution.py:107
  20.4 3.9 %collective-permute-start = (bf16[256,512]{1,0:T(8,128)(2,1)S(1)}, bf16[256,512]{1,0:T(8,128)(2,1)S(1)}, u32[]{:S(2)}, u32[]{:S(2)}) collective-permute-start(bf16[256,512]{1,0:T(8,128)(2,1)S(1)} %get-tuple-element.122), channel_id=1, source_target_pairs={{128,192},{256,320},{0,64},{192,256},{129,193},{257,321},{1,65},{1... | collective-permute-start | bytes 786440 | tf_op jit(solution)/shard_map/cond/branch_0_fun/ppermute | solution.py:107
  24.4 0.8 reduce-window.40
  25.2 1.3 %fusion.141 = (s32[]{:T(128)}, s32[4]{0:T(128)S(1)}) fusion(s32[4]{0:T(128)} %get-tuple-element.74, s32[4,1]{0,1:T(1,128)S(1)} %reduce-window.40), kind=kLoop, calls=%fused_computation.264 | loop fusion | flops 7 | bytes 52 | tf_op jit(solution)/shard_map/cond/branch_0_fun/reduce_sum | solution.py:167
  26.5 0.0 copy-start.5
  26.5 3.6 %fusion.6 = f32[512,1024]{1,0:T(8,128)} fusion(bf16[512,512]{1,0:T(8,128)(2,1)} %get-tuple-element.72, bf16[2,512,1024]{2,1,0:T(8,128)(2,1)} %get-tuple-element.75), kind=kOutput, calls=%fused_computation.19 | convolution fusion | flops 536870912 | bytes 3670016 | tf_op jit(solution)/shard_map/cond/branch_0_fun/dot_general | solution.py:161
  30.1 0.1 select_reduce_fusion
  30.2 0.7 compare_and_fusion
  30.8 0.0 collective-permute-done.1
  30.8 0.7 collective-permute-start.2
  31.5 0.7 fusion.21
  32.2 0.7 fusion.23
  32.9 19.4 %collective-permute-done.3 = bf16[256,512]{1,0:T(8,128)(2,1)S(1)} collective-permute-done((bf16[256,512]{1,0:T(8,128)(2,1)S(1)}, bf16[256,512]{1,0:T(8,128)(2,1)S(1)}, u32[]{:S(2)}, u32[]{:S(2)}) %collective-permute-start.3) | collective-permute-done | bytes 262176 | tf_op jit(solution)/shard_map/cond/branch_0_fun/ppermute | solution.py:107
  52.3 0.0 collective-permute-done.2
  52.4 5.6 %collective-permute-done = bf16[256,512]{1,0:T(8,128)(2,1)S(1)} collective-permute-done((bf16[256,512]{1,0:T(8,128)(2,1)S(1)}, bf16[256,512]{1,0:T(8,128)(2,1)S(1)}, u32[]{:S(2)}, u32[]{:S(2)}) %collective-permute-start) | collective-permute-done | bytes 262176 | tf_op jit(solution)/shard_map/cond/branch_0_fun/ppermute | solution.py:107
  58.0 0.2 maximum_select_fusion
  58.2 0.0 copy-done.5
  58.2 0.0 copy-start.10
  58.2 0.0 copy-start.15
  58.2 2.4 %convolution_add_fusion = f32[512,1024]{1,0:T(8,128)S(1)} fusion(f32[512,1024]{1,0:T(8,128)} %fusion.6, bf16[512,512]{1,0:T(8,128)(2,1)S(1)} %maximum_select_fusion, bf16[2,512,1024]{2,1,0:T(8,128)(2,1)S(1)} %copy-done.5), kind=kOutput, calls=%fused_computation | convolution fusion | flops 537395200 | bytes 5767168 | tf_op jit(solution)/shard_map/cond/branch_0_fun/dot_general | solution.py:173
  60.6 0.0 copy-done.10
  60.6 0.0 copy-done.15
  60.7 0.8 multiply_convert_fusion.1
  61.5 0.5 fusion.1
  62.0 0.0 copy-start
  62.0 1.4 %collective-permute-start.8 = (bf16[256,512]{1,0:T(8,128)(2,1)S(1)}, bf16[256,512]{1,0:T(8,128)(2,1)S(1)}, u32[]{:S(2)}, u32[]{:S(2)}) collective-permute-start(bf16[256,512]{1,0:T(8,128)(2,1)S(1)} %fusion.1), channel_id=1, source_target_pairs={{192,128},{320,256},{193,129},{321,257},{194,130},{322,258},{195,1... | collective-permute-start | bytes 786440 | tf_op jit(solution)/shard_map/cond/branch_0_fun/ppermute | solution.py:107
  63.5 0.7 collective-permute-start.6
  64.1 0.5 fusion
  64.6 1.3 %collective-permute-start.5 = (bf16[256,512]{1,0:T(8,128)(2,1)S(1)}, bf16[256,512]{1,0:T(8,128)(2,1)S(1)}, u32[]{:S(2)}, u32[]{:S(2)}) collective-permute-start(bf16[256,512]{1,0:T(8,128)(2,1)S(1)} %fusion), channel_id=1, source_target_pairs={{192,128},{320,256},{64,0},{193,129},{321,257},{65,1},{194,130},{3... | collective-permute-start | bytes 786440 | tf_op jit(solution)/shard_map/cond/branch_0_fun/ppermute | solution.py:107
  65.9 0.7 collective-permute-start.4
  66.6 0.0 copy-done
  66.6 1.5 %convolution_add_fusion.2 = bf16[512,512]{1,0:T(8,128)(2,1)} fusion(bf16[512,512]{1,0:T(8,128)(2,1)S(1)} %copy-done.10, bf16[512,512]{1,0:T(8,128)(2,1)S(1)} %copy-done, f32[512,1024]{1,0:T(8,128)S(1)} %convolution_add_fusion, f32[512]{0:T(512)S(1)} %fusion.23), kind=kOutput, calls=%fused_computation.3 | convolution fusion | flops 270794752 | bytes 3672064 | tf_op jit(solution)/shard_map/cond/branch_0_fun/dot_general | solution.py:192
  68.1 0.0 collective-permute-done.6
  68.1 0.7 collective-permute-start.7
  68.8 0.8 convolution_add_fusion.1
  69.6 38.4 %collective-permute-done.5 = bf16[256,512]{1,0:T(8,128)(2,1)S(1)} collective-permute-done((bf16[256,512]{1,0:T(8,128)(2,1)S(1)}, bf16[256,512]{1,0:T(8,128)(2,1)S(1)}, u32[]{:S(2)}, u32[]{:S(2)}) %collective-permute-start.5) | collective-permute-done | bytes 262176 | tf_op jit(solution)/shard_map/cond/branch_0_fun/ppermute | solution.py:107
  108.0 0.0 collective-permute-done.4
  108.0 0.0 collective-permute-done.8
  108.0 0.0 collective-permute-done.7
  108.1 1.0 convert_add_fusion
  (5 shorter events, 0.1 us)
Async XLA Ops:
  3.6 48.7 %collective-permute-start.3 = (bf16[256,512]{1,0:T(8,128)(2,1)S(1)}, bf16[256,512]{1,0:T(8,128)(2,1)S(1)}, u32[]{:S(2)}, u32[]{:S(2)}) collective-permute-start(bf16[256,512]{1,0:T(8,128)(2,1)S(1)} %get-tuple-element.123), channel_id=1, source_target_pairs={{128,192},{256,320},{129,193},{257,321},{130,194},{258,322},{131,1... | collective-permute-start | bytes 786440 | tf_op jit(solution)/shard_map/cond/branch_0_fun/ppermute | solution.py:107
  19.1 11.8 %collective-permute-start.1 = (bf16[256,512]{1,0:T(8,128)(2,1)S(1)}, bf16[256,512]{1,0:T(8,128)(2,1)}, u32[]{:S(2)}, u32[]{:S(2)}) collective-permute-start(bf16[256,512]{1,0:T(8,128)(2,1)S(1)} %get-tuple-element.123), channel_id=1, source_target_pairs={{0,384},{192,448},{1,385},{193,449},{2,386},{194,450},{3,387},{195... | collective-permute-start | bytes 786440 | tf_op jit(solution)/shard_map/cond/branch_0_fun/ppermute | solution.py:107
  20.4 37.5 %collective-permute-start = (bf16[256,512]{1,0:T(8,128)(2,1)S(1)}, bf16[256,512]{1,0:T(8,128)(2,1)S(1)}, u32[]{:S(2)}, u32[]{:S(2)}) collective-permute-start(bf16[256,512]{1,0:T(8,128)(2,1)S(1)} %get-tuple-element.122), channel_id=1, source_target_pairs={{128,192},{256,320},{0,64},{192,256},{129,193},{257,321},{1,65},{1... | collective-permute-start | bytes 786440 | tf_op jit(solution)/shard_map/cond/branch_0_fun/ppermute | solution.py:107
  26.5 31.7 %copy-start.5 = (bf16[2,512,1024]{2,1,0:T(8,128)(2,1)S(1)}, bf16[2,512,1024]{2,1,0:T(8,128)(2,1)}, u32[]{:S(2)}) copy-start(bf16[2,512,1024]{2,1,0:T(8,128)(2,1)} %get-tuple-element.75) | copy-start | bytes 6291460
  30.8 21.5 %collective-permute-start.2 = (bf16[256,512]{1,0:T(8,128)(2,1)}, bf16[256,512]{1,0:T(8,128)(2,1)S(1)}, u32[]{:S(2)}, u32[]{:S(2)}) collective-permute-start(bf16[256,512]{1,0:T(8,128)(2,1)} %collective-permute-done.1), channel_id=1, source_target_pairs={{384,64},{448,256},{385,65},{449,257},{386,66},{450,258},{387,67},... | collective-permute-start | bytes 786440 | tf_op jit(solution)/shard_map/cond/branch_0_fun/ppermute | solution.py:107
  58.2 2.5 %copy-start.10 = (bf16[512,512]{1,0:T(8,128)(2,1)S(1)}, bf16[512,512]{1,0:T(8,128)(2,1)}, u32[]{:S(2)}) copy-start(bf16[512,512]{1,0:T(8,128)(2,1)} %get-tuple-element.76) | copy-start | bytes 1572868
  58.2 2.5 %copy-start.15 = (bf16[512,512]{1,0:T(8,128)(2,1)S(1)}, bf16[512,512]{1,0:T(8,128)(2,1)}, u32[]{:S(2)}) copy-start(bf16[512,512]{1,0:T(8,128)(2,1)} %get-tuple-element.77) | copy-start | bytes 1572868
  62.0 4.6 %copy-start = (bf16[512,512]{1,0:T(8,128)(2,1)S(1)}, bf16[512,512]{1,0:T(8,128)(2,1)}, u32[]{:S(2)}) copy-start(bf16[512,512]{1,0:T(8,128)(2,1)} %get-tuple-element.72) | copy-start | bytes 1572868
  62.0 46.0 %collective-permute-start.8 = (bf16[256,512]{1,0:T(8,128)(2,1)S(1)}, bf16[256,512]{1,0:T(8,128)(2,1)S(1)}, u32[]{:S(2)}, u32[]{:S(2)}) collective-permute-start(bf16[256,512]{1,0:T(8,128)(2,1)S(1)} %fusion.1), channel_id=1, source_target_pairs={{192,128},{320,256},{193,129},{321,257},{194,130},{322,258},{195,1... | collective-permute-start | bytes 786440 | tf_op jit(solution)/shard_map/cond/branch_0_fun/ppermute | solution.py:107
  63.5 4.7 %collective-permute-start.6 = (bf16[256,512]{1,0:T(8,128)(2,1)S(1)}, bf16[256,512]{1,0:T(8,128)(2,1)S(1)}, u32[]{:S(2)}, u32[]{:S(2)}) collective-permute-start(bf16[256,512]{1,0:T(8,128)(2,1)S(1)} %fusion.1), channel_id=1, source_target_pairs={{64,448},{256,384},{65,449},{257,385},{66,450},{258,386},{67,451},... | collective-permute-start | bytes 786440 | tf_op jit(solution)/shard_map/cond/branch_0_fun/ppermute | solution.py:107
  64.6 43.3 %collective-permute-start.5 = (bf16[256,512]{1,0:T(8,128)(2,1)S(1)}, bf16[256,512]{1,0:T(8,128)(2,1)S(1)}, u32[]{:S(2)}, u32[]{:S(2)}) collective-permute-start(bf16[256,512]{1,0:T(8,128)(2,1)S(1)} %fusion), channel_id=1, source_target_pairs={{192,128},{320,256},{64,0},{193,129},{321,257},{65,1},{194,130},{3... | collective-permute-start | bytes 786440 | tf_op jit(solution)/shard_map/cond/branch_0_fun/ppermute | solution.py:107
  65.9 42.0 %collective-permute-start.4 = (bf16[256,512]{1,0:T(8,128)(2,1)S(1)}, bf16[256,512]{1,0:T(8,128)(2,1)S(1)}, u32[]{:S(2)}, u32[]{:S(2)}) collective-permute-start(bf16[256,512]{1,0:T(8,128)(2,1)S(1)} %fusion), channel_id=1, source_target_pairs={{256,192},{257,193},{258,194},{259,195},{260,196},{261,197},{262,1... | collective-permute-start | bytes 786440 | tf_op jit(solution)/shard_map/cond/branch_0_fun/ppermute | solution.py:107
  68.1 39.9 %collective-permute-start.7 = (bf16[256,512]{1,0:T(8,128)(2,1)S(1)}, bf16[256,512]{1,0:T(8,128)(2,1)S(1)}, u32[]{:S(2)}, u32[]{:S(2)}) collective-permute-start(bf16[256,512]{1,0:T(8,128)(2,1)S(1)} %collective-permute-done.6), channel_id=1, source_target_pairs={{448,0},{384,192},{449,1},{385,193},{450,2},{386,194},{451,3},{387... | collective-permute-start | bytes 786440 | tf_op jit(solution)/shard_map/cond/branch_0_fun/ppermute | solution.py:107
